TPU v7x, 32 devices: a whole 2x2x4 slice. The times are simulated.
32 devices in a mesh: group: 4 (over x, core), member: 8 (over z, y).
Axes of the slice: x: 2, y: 2, z: 4, core: 2. Of those that a mesh axis runs over, the one named last changes fastest.
Arguments:
- activations: bfloat16 [8192, 1152], P(('group', 'member')), may hold values from -6 to 6
- routes: int32 [8192, 1], P(('group', 'member')), may hold values from 0 to 31; in each aligned block of 256 rows (0 to 255, 256 to 511, ...) at most 16 rows name the same one
- centre_bias: float32 [1152], replicated, may hold values from -2 to 2
- centre_first: float32 [1152], replicated, may hold values from -600 to 600
- centre_second: float32 [1152], replicated, may hold values from 1000 to 1000000
- router: bfloat16 [32, 1152], P(('group', 'member')), may hold values from -0.1875 to 0.1875
- router_first: float32 [32, 1152], P(('group', 'member')), may hold values from -180 to 180
- router_second: float32 [32, 1152], P(('group', 'member')), may hold values from 100 to 100000
- encoder: bfloat16 [32, 1152, 512], P(('group', 'member')), may hold values from -0.1875 to 0.1875
- enc_bias: float32 [32, 512], P(('group', 'member')), may hold values from -3 to 3
- decoder: bfloat16 [32, 512, 1152], P(('group', 'member')), may hold values from -0.25 to 0.25
- encoder_first: float32 [32, 1152, 512], P(('group', 'member')), may hold values from -30 to 30
- encoder_second: float32 [32, 1152, 512], P(('group', 'member')), may hold values from 1 to 1000
- enc_bias_first: float32 [32, 512], P(('group', 'member')), may hold values from -60 to 60
- enc_bias_second: float32 [32, 512], P(('group', 'member')), may hold values from 10 to 10000
- decoder_first: float32 [32, 512, 1152], P(('group', 'member')), may hold values from -30 to 30
- decoder_second: float32 [32, 512, 1152], P(('group', 'member')), may hold values from 1 to 1000
Outputs:
- recon: bfloat16 [8192, 1152], P(('group', 'member'))
- new_centre: float32 [1152], replicated
- new_centre_first: float32 [1152], replicated
- new_centre_second: float32 [1152], replicated
- new_router: bfloat16 [32, 1152], P(('group', 'member'))
- new_router_first: float32 [32, 1152], P(('group', 'member'))
- new_router_second: float32 [32, 1152], P(('group', 'member'))
- new_encoder: bfloat16 [32, 1152, 512], P(('group', 'member'))
- new_enc_bias: float32 [32, 512], P(('group', 'member'))
- new_decoder: bfloat16 [32, 512, 1152], P(('group', 'member'))
- new_encoder_first: float32 [32, 1152, 512], P(('group', 'member'))
- new_encoder_second: float32 [32, 1152, 512], P(('group', 'member'))
- new_enc_bias_first: float32 [32, 512], P(('group', 'member'))
- new_enc_bias_second: float32 [32, 512], P(('group', 'member'))
- new_decoder_first: float32 [32, 512, 1152], P(('group', 'member'))
- new_decoder_second: float32 [32, 512, 1152], P(('group', 'member'))
Inputs may be any that keep to these rules, and one draw needn't show every extreme that they name: `routes`: each row names the one expert that serves it. At most 16 rows of one device name the same expert, and in every draw some device's rows name some expert exactly 16 times.
All inputs are finite; a program needn't handle non-finite values.
Results may differ from a plain program's by a relative error of at most 0.009.
Values may be sent and summed in bfloat16 or wider, within the bound.
A program may use at most 128 MiB of HBM per device.

v0:
```python
import jax
import jax.numpy as jnp
from jax import lax
from jax.sharding import PartitionSpec as P

STEP = 10


learn_rate = 0.001
beta_one = 0.9
beta_two = 0.999
adam_eps = 1e-08
sparsity = 0.1


def adam_update(weights_in, gradient, moment_one, moment_two):
    first_new = beta_one * moment_one + (1.0 - beta_one) * gradient
    second_new = beta_two * moment_two + (1.0 - beta_two) * gradient * gradient
    first_hat = first_new / (1.0 - beta_one**STEP)
    second_hat = second_new / (1.0 - beta_two**STEP)
    stepped = weights_in.astype(jnp.float32) - learn_rate * first_hat / (
        jnp.sqrt(second_hat) + adam_eps
    )
    return (stepped.astype(weights_in.dtype), first_new, second_new)


def forward_pass(in_rows, centre_bias, router_row, encoder, enc_bias, decoder):
    centred = (in_rows.astype(jnp.float32) - centre_bias).astype(jnp.bfloat16)
    preact = jnp.dot(centred, encoder, preferred_element_type=jnp.float32) + enc_bias
    positive = jnp.maximum(preact, 0.0)
    latents = (positive * positive).astype(jnp.bfloat16)
    logits = jnp.dot(in_rows, router_row, preferred_element_type=jnp.float32)
    gating = jax.nn.sigmoid(logits)
    ungated = jnp.dot(latents, decoder, preferred_element_type=jnp.float32)
    rebuilt = centre_bias + gating[:, None] * ungated
    return (centred, positive, latents, gating, ungated, rebuilt)


def backward_pass(
    in_rows, live_mask, centred, positive, latents, gating, ungated, rebuilt, encoder, decoder
):
    errors = (in_rows.astype(jnp.float32) - rebuilt) * live_mask[:, None]
    backward = (-gating[:, None] * errors).astype(jnp.bfloat16)
    decoder_grad = jnp.dot(latents.T, backward, preferred_element_type=jnp.float32)
    latent_grad = jnp.dot(backward, decoder.T, preferred_element_type=jnp.float32) + sparsity
    preact_grad = (latent_grad * 2.0 * positive * live_mask[:, None]).astype(jnp.bfloat16)
    encoder_grad = jnp.dot(centred.T, preact_grad, preferred_element_type=jnp.float32)
    bias_grad = jnp.sum(preact_grad.astype(jnp.float32), axis=0)
    logit_grad = (-jnp.sum(errors * ungated, axis=1) * gating * (1.0 - gating)).astype(jnp.bfloat16)
    router_grad = jnp.dot(logit_grad, in_rows, preferred_element_type=jnp.float32)
    centre_part = -jnp.sum(errors, axis=0) - jnp.dot(
        encoder.astype(jnp.float32), bias_grad, precision=lax.Precision.HIGHEST
    )
    return (encoder_grad, bias_grad, decoder_grad, router_grad, centre_part)


def per_device(
    activations,
    routes,
    centre_bias,
    centre_first,
    centre_second,
    router,
    router_first,
    router_second,
    encoder,
    enc_bias,
    decoder,
    encoder_first,
    encoder_second,
    enc_bias_first,
    enc_bias_second,
    decoder_first,
    decoder_second,
):
    groups = lax.axis_size("group")
    members = lax.axis_size("member")
    devices = groups * members
    row_count = activations.shape[0]
    feature_count = activations.shape[1]
    slot_cap = 2 * row_count // devices
    route_ids = routes[:, 0]
    onehot = (route_ids[:, None] == jnp.arange(devices, dtype=jnp.int32)[None, :]).astype(
        jnp.float32
    )
    earlier = (jnp.arange(row_count)[:, None] > jnp.arange(row_count)[None, :]).astype(jnp.float32)
    before = jnp.dot(earlier, onehot, precision=lax.Precision.HIGHEST)
    slot_rank = jnp.sum(before * onehot, axis=1).astype(jnp.int32)
    position = route_ids * slot_cap + slot_rank
    packed = (
        jnp.zeros((devices * slot_cap, feature_count), jnp.bfloat16).at[position].set(activations)
    )
    filled = (
        jnp.zeros((devices * slot_cap,), jnp.bfloat16)
        .at[position]
        .set(jnp.ones((row_count,), jnp.bfloat16))
    )
    arrived, arrived_mask = (
        lax.all_to_all(
            packed.reshape(devices, slot_cap, feature_count),
            ("group", "member"),
            split_axis=0,
            concat_axis=0,
            tiled=True,
        ),
        lax.all_to_all(
            filled.reshape(devices, slot_cap),
            ("group", "member"),
            split_axis=0,
            concat_axis=0,
            tiled=True,
        ),
    )
    in_rows = arrived.reshape(devices * slot_cap, feature_count)
    live_mask = arrived_mask.reshape(devices * slot_cap).astype(jnp.float32)
    centred, positive, latents, gating, ungated, rebuilt = forward_pass(
        in_rows, centre_bias, router[0], encoder[0], enc_bias[0], decoder[0]
    )
    outgoing = rebuilt.astype(jnp.bfloat16)
    returned = lax.all_to_all(
        outgoing.reshape(devices, slot_cap, feature_count),
        ("group", "member"),
        split_axis=0,
        concat_axis=0,
        tiled=True,
    )
    recon = returned.reshape(devices * slot_cap, feature_count)[position]
    encoder_grad, bias_grad, decoder_grad, router_grad, centre_part = backward_pass(
        in_rows,
        live_mask,
        centred,
        positive,
        latents,
        gating,
        ungated,
        rebuilt,
        encoder[0],
        decoder[0],
    )
    router_new = adam_update(router[0], router_grad, router_first[0], router_second[0])
    encoder_new = adam_update(encoder[0], encoder_grad, encoder_first[0], encoder_second[0])
    bias_new = adam_update(enc_bias[0], bias_grad, enc_bias_first[0], enc_bias_second[0])
    decoder_new = adam_update(decoder[0], decoder_grad, decoder_first[0], decoder_second[0])
    centre_total = lax.psum(centre_part, ("group", "member"))
    centre_new = adam_update(centre_bias, centre_total, centre_first, centre_second)
    return (
        recon,
        centre_new[0],
        centre_new[1],
        centre_new[2],
        router_new[0][None],
        router_new[1][None],
        router_new[2][None],
        encoder_new[0][None],
        bias_new[0][None],
        decoder_new[0][None],
        encoder_new[1][None],
        encoder_new[2][None],
        bias_new[1][None],
        bias_new[2][None],
        decoder_new[1][None],
        decoder_new[2][None],
    )


def solution(mesh):
    placed = (
        P(("group", "member"), None),
        P(("group", "member"), None),
        P(),
        P(),
        P(),
        P(("group", "member"), None),
        P(("group", "member"), None),
        P(("group", "member"), None),
        P(("group", "member"), None, None),
        P(("group", "member"), None),
        P(("group", "member"), None, None),
        P(("group", "member"), None, None),
        P(("group", "member"), None, None),
        P(("group", "member"), None),
        P(("group", "member"), None),
        P(("group", "member"), None, None),
        P(("group", "member"), None, None),
    )
    return jax.shard_map(
        per_device,
        mesh=mesh,
        in_specs=placed,
        out_specs=(
            P(("group", "member"), None),
            P(),
            P(),
            P(),
            P(("group", "member"), None),
            P(("group", "member"), None),
            P(("group", "member"), None),
            P(("group", "member"), None, None),
            P(("group", "member"), None),
            P(("group", "member"), None, None),
            P(("group", "member"), None, None),
            P(("group", "member"), None, None),
            P(("group", "member"), None),
            P(("group", "member"), None),
            P(("group", "member"), None, None),
            P(("group", "member"), None, None),
        ),
        check_vma=False,
    )
```

profile of v0, /device:TPU:0, one launch (start us, length us, event | category | flops | bytes accessed | tf_op | source)
XLA Modules:
  0.0 127.9 jit_solution(12452941034543054141)
XLA Ops:
  0.7 1.0 fusion.22
  1.6 0.7 compare_select_fusion
  2.3 2.2 %scatter_custom_fusion.1 = bf16[512]{0:T(512)(128)(2,1)S(1)} fusion(s32[256]{0:T(256)S(1)} %bitcast.95, bf16[256]{0:T(256)(128)(2,1)S(1)} %broadcast.120, bf16[]{:T(256)} %constant.17.clone.1), kind=kCustom, calls=%fused_computation.76 | custom fusion | bytes 1026 | tf_op jit(solution)/shard_map/scatter | solution.py:96
  4.5 0.7 all_to_all.16
  5.2 7.3 %all-to-all-start.2 = ((bf16[32,1,16]{2,1,0:T(2,128)(2,1)}), bf16[32,1,16]{2,1,0:T(2,128)(2,1)S(1)}, u32[]{:S(2)}, u32[]{:S(2)}) async-start(bf16[32,1,16]{2,1,0:T(2,128)(2,1)} %all_to_all.16), calls=%async_computation.2 | async-start | bytes 32768 | tf_op jit(solution)/shard_map/all_to_all | solution.py:106
  12.5 3.4 %scatter_custom_fusion = bf16[512,1152]{1,0:T(8,128)(2,1)} fusion(s32[256]{0:T(256)S(1)} %bitcast.96, bf16[256,1152]{1,0:T(8,128)(2,1)} %param.17, bf16[]{:T(256)} %constant.17.clone.1), kind=kCustom, calls=%fused_computation.48 | custom fusion | bytes 1180160 | tf_op jit(solution)/shard_map/scatter | solution.py:91
  15.9 3.7 %all-to-all-done.2 = bf16[32,1,16]{2,1,0:T(2,128)(2,1)S(1)} async-done(((bf16[32,1,16]{2,1,0:T(2,128)(2,1)}), bf16[32,1,16]{2,1,0:T(2,128)(2,1)S(1)}, u32[]{:S(2)}, u32[]{:S(2)}) %all-to-all-start.2) | async-done | bytes 1056 | tf_op jit(solution)/shard_map/all_to_all | solution.py:106
  19.6 2.7 %all-to-all-start = ((bf16[32,16,1152]{2,1,0:T(8,128)(2,1)}), bf16[32,16,1152]{2,1,0:T(8,128)(2,1)S(1)}, u32[]{:S(2)}, u32[]{:S(2)}) async-start(bf16[32,16,1152]{2,1,0:T(8,128)(2,1)} %bitcast.3), calls=%async_computation | async-start | bytes 2359296 | tf_op jit(solution)/shard_map/all_to_all | solution.py:99
  22.3 0.6 reduce.2
  23.5 0.6 multiply_reduce_fusion.1
  24.3 28.3 %all-to-all-done = bf16[32,16,1152]{2,1,0:T(8,128)(2,1)S(1)} async-done(((bf16[32,16,1152]{2,1,0:T(8,128)(2,1)}), bf16[32,16,1152]{2,1,0:T(8,128)(2,1)S(1)}, u32[]{:S(2)}, u32[]{:S(2)}) %all-to-all-start) | async-done | bytes 1179680 | tf_op jit(solution)/shard_map/all_to_all | solution.py:99
  53.3 0.9 fusion.8
  54.5 3.2 %multiply_reduce_fusion = (f32[512]{0:T(512)S(1)}, f32[1152]{0:T(1024)}, bf16[512,1152]{1,0:T(8,128)(2,1)}, bf16[512,1152]{1,0:T(8,128)(2,1)}) fusion(f32[512]{0:T(512)S(1)} %reshape.108, f32[512]{0:T(512)S(1)} %get-tuple-element.28, f32[1152]{0:T(1024)S(1)} %copy-done.1, bf16[32,16,1152]{2,1,0:T(8,128)(2,1)S(1)} %all-to-all-done, ...), kind=kOutput, calls=%fused_computation.15 | convolution fusion | flops 610990464 | bytes 5784576 | tf_op jit(solution)/shard_map/dot_general | solution.py:34
  58.1 2.7 %all-to-all-start.1 = ((bf16[32,16,1152]{2,1,0:T(8,128)(2,1)}), bf16[32,16,1152]{2,1,0:T(8,128)(2,1)S(1)}, u32[]{:S(2)}, u32[]{:S(2)}) async-start(bf16[32,16,1152]{2,1,0:T(8,128)(2,1)} %bitcast.90), calls=%async_computation.1 | async-start | bytes 2359296 | tf_op jit(solution)/shard_map/all_to_all | solution.py:120
  60.8 3.7 %convert_reduce_fusion = (f32[512]{0:T(512)S(1)}, bf16[512,512]{1,0:T(8,128)(2,1)}) fusion(f32[512]{0:T(512)} %copy-done.11, f32[512,512]{1,0:T(8,128)} %copy-done.15, bf16[512,1152]{1,0:T(8,128)(2,1)} %get-tuple-element.35, bf16[1,512,1152]{2,1,0:T(8,128)(2,1)} %param.27), kind=kOutput, calls=%fused_computation.42 | convolution fusion | flops 605814272 | bytes 3936256 | tf_op jit(solution)/shard_map/dot_general | solution.py:45
  64.5 1.0 fusion.23
  65.6 0.6 broadcast_in_dim.54
  67.4 0.6 negate_subtract_fusion
  68.0 41.9 %psum.7 = f32[1152]{0:T(1024)S(1)} all-reduce(f32[1152]{0:T(1024)} %negate_subtract_fusion), channel_id=1, replica_groups=mesh['group'=4,'member'=8] {'group','member'}, use_global_device_ids=true, to_apply=%region_5.0 | all-reduce | flops 1152 | bytes 9216 | tf_op jit(solution)/shard_map/psum | solution.py:144
  109.9 1.3 %divide_subtract_fusion.1 = (f32[1,512]{1,0:T(1,128)}, f32[1,512]{1,0:T(1,128)}, f32[1,512]{1,0:T(1,128)}) fusion(f32[1,512]{1,0:T(1,128)} %param.26, f32[1,512]{1,0:T(1,128)} %bitcast.93, f32[1,512]{1,0:T(1,128)} %param.30, f32[1,512]{1,0:T(1,128)} %param.31), kind=kLoop, calls=%fused_computation.72 | loop fusion | flops 6144 | bytes 14336 | tf_op jit(solution)/shard_map/sub | solution.py:21
  111.2 1.3 %divide_subtract_fusion = (f32[1152]{0:T(1024)}, f32[1152]{0:T(1024)}, f32[1152]{0:T(1024)}) fusion(f32[1152]{0:T(1024)S(1)} %copy-done.1, f32[1152]{0:T(1024)S(1)} %psum.7, f32[1152]{0:T(1024)} %param.20, f32[1152]{0:T(1024)} %param.21), kind=kLoop, calls=%fused_computation.61 | loop fusion | flops 13824 | bytes 32256 | tf_op jit(solution)/shard_map/sub | solution.py:21
  112.6 8.3 %fusion.28 = (f32[1,512,1152]{2,1,0:T(8,128)}, bf16[1,512,1152]{2,1,0:T(8,128)(2,1)}, f32[1,512,1152]{2,1,0:T(8,128)}) fusion(f32[1,512,1152]{2,1,0:T(8,128)} %param.33, f32[1,512,1152]{2,1,0:T(8,128)} %param.32, bf16[1,512,1152]{2,1,0:T(8,128)(2,1)} %param.27, bf16[512,1152]{1,0:T(8,128)(2,1)} %get-tuple-element.35, f32[512,512]{1,0:T(8,128)} %copy-done.15), kind=kOutput, calls=%fused_computation.46 | convolution fusion | flops 612761600 | bytes 14024704 | tf_op jit(solution)/shard_map/dot_general | solution.py:44
  120.9 4.8 %fusion.29 = (f32[1,1152,512]{2,1,0:T(8,128)}, bf16[1,1152,512]{2,1,0:T(8,128)(2,1)}, f32[1,1152,512]{2,1,0:T(8,128)}) fusion(f32[1,1152,512]{2,1,0:T(8,128)S(1)} %copy-done.12, f32[1,1152,512]{2,1,0:T(8,128)S(1)} %copy-done.13, bf16[1,1152,512]{2,1,0:T(8,128)(2,1)S(1)} %copy-done, bf16[512,512]{1,0:T(8,128)(2,1)S(1)} %copy-done.16, ...), kind=kOutput, calls=%fused_computation.47 | convolution fusion | flops 614006784 | bytes 13505024 | tf_op jit(solution)/shard_map/dot_general | solution.py:47
  125.7 2.2 %gather_fusion = bf16[256,1152]{1,0:T(8,128)(2,1)} fusion(bf16[512,1152]{1,0:T(8,128)(2,1)S(1)} %bitcast.86, s32[1024]{0:T(1024)} %pad_clamp_fusion), kind=kCustom, calls=%fused_computation | custom fusion | bytes 1180672 | tf_op jit(solution)/shard_map/gather | solution.py:127
  (49 shorter events, 3.3 us)
Async XLA Ops:
  0.6 21.6 %copy-start.4 = (bf16[1,1152]{1,0:T(2,128)(2,1)S(1)}, bf16[1,1152]{1,0:T(2,128)(2,1)}, u32[]{:S(2)}) copy-start(bf16[1,1152]{1,0:T(2,128)(2,1)} %param.22) | copy-start | bytes 6916
  0.7 22.9 %copy-start.8 = (f32[1,1152]{1,0:T(1,128)S(1)}, f32[1,1152]{1,0:T(1,128)}, u32[]{:S(2)}) copy-start(f32[1,1152]{1,0:T(1,128)} %param.24) | copy-start | bytes 13828
  0.7 22.9 %copy-start.9 = (f32[1,1152]{1,0:T(1,128)S(1)}, f32[1,1152]{1,0:T(1,128)}, u32[]{:S(2)}) copy-start(f32[1,1152]{1,0:T(1,128)} %param.23) | copy-start | bytes 13828
  5.2 14.4 %all-to-all-start.2 = ((bf16[32,1,16]{2,1,0:T(2,128)(2,1)}), bf16[32,1,16]{2,1,0:T(2,128)(2,1)S(1)}, u32[]{:S(2)}, u32[]{:S(2)}) async-start(bf16[32,1,16]{2,1,0:T(2,128)(2,1)} %all_to_all.16), calls=%async_computation.2 | async-start | bytes 32768 | tf_op jit(solution)/shard_map/all_to_all | solution.py:106
  12.5 40.5 %copy-start.1 = (f32[1152]{0:T(1024)S(1)}, f32[1152]{0:T(1024)}, u32[]{:S(2)}) copy-start(f32[1152]{0:T(1024)} %param.19) | copy-start | bytes 13828
  19.6 33.0 %all-to-all-start = ((bf16[32,16,1152]{2,1,0:T(8,128)(2,1)}), bf16[32,16,1152]{2,1,0:T(8,128)(2,1)S(1)}, u32[]{:S(2)}, u32[]{:S(2)}) async-start(bf16[32,16,1152]{2,1,0:T(8,128)(2,1)} %bitcast.3), calls=%async_computation | async-start | bytes 2359296 | tf_op jit(solution)/shard_map/all_to_all | solution.py:99
  22.3 30.9 %copy-start = (bf16[1,1152,512]{2,1,0:T(8,128)(2,1)S(1)}, bf16[1,1152,512]{2,1,0:T(8,128)(2,1)}, u32[]{:S(2)}) copy-start(bf16[1,1152,512]{2,1,0:T(8,128)(2,1)} %param.25) | copy-start | bytes 3538948
  22.3 30.9 %copy-start.10 = (f32[1,512]{1,0:T(1,128)S(1)}, f32[1,512]{1,0:T(1,128)}, u32[]{:S(2)}) copy-start(f32[1,512]{1,0:T(1,128)} %param.26) | copy-start | bytes 6148
  24.3 29.8 %copy-start.11 = (f32[512]{0:T(512)}, f32[512]{0:T(512)S(1)}, u32[]{:S(2)}) copy-start(f32[512]{0:T(512)S(1)} %reshape.108) | copy-start | bytes 6148
  53.2 1.3 copy-start.14
  54.1 3.7 %copy-start.15 = (f32[512,512]{1,0:T(8,128)}, f32[512,512]{1,0:T(8,128)S(1)}, u32[]{:S(2)}) copy-start(f32[512,512]{1,0:T(8,128)S(1)} %fusion.8) | copy-start | bytes 3145732
  58.1 67.7 %all-to-all-start.1 = ((bf16[32,16,1152]{2,1,0:T(8,128)(2,1)}), bf16[32,16,1152]{2,1,0:T(8,128)(2,1)S(1)}, u32[]{:S(2)}, u32[]{:S(2)}) async-start(bf16[32,16,1152]{2,1,0:T(8,128)(2,1)} %bitcast.90), calls=%async_computation.1 | async-start | bytes 2359296 | tf_op jit(solution)/shard_map/all_to_all | solution.py:120
  60.7 3.7 %copy-start.2 = (f32[1152]{0:T(1024)S(1)}, f32[1152]{0:T(1024)}, u32[]{:S(2)}) copy-start(f32[1152]{0:T(1024)} %get-tuple-element.39) | copy-start | bytes 13828
  60.7 3.7 %copy-start.3 = (f32[1152]{0:T(1024)S(1)}, f32[1152]{0:T(1024)}, u32[]{:S(2)}) copy-start(f32[1152]{0:T(1024)} %get-tuple-element.40) | copy-start | bytes 13828
  60.8 3.7 %copy-start.5 = (bf16[1152]{0:T(1024)(128)(2,1)S(1)}, bf16[1152]{0:T(1024)(128)(2,1)}, u32[]{:S(2)}) copy-start(bf16[1152]{0:T(1024)(128)(2,1)} %reduce.2) | copy-start | bytes 6916
  60.8 6.6 %copy-start.7 = (f32[1152]{0:T(1024)S(1)}, f32[1152]{0:T(1024)}, u32[]{:S(2)}) copy-start(f32[1152]{0:T(1024)} %get-tuple-element.17) | copy-start | bytes 13828
  64.5 2.9 %copy-start.6 = (f32[512]{0:T(512)}, f32[512]{0:T(512)S(1)}, u32[]{:S(2)}) copy-start(f32[512]{0:T(512)S(1)} %get-tuple-element.37) | copy-start | bytes 6148
  112.5 8.3 %copy-start.12 = (f32[1,1152,512]{2,1,0:T(8,128)S(1)}, f32[1,1152,512]{2,1,0:T(8,128)}, u32[]{:S(2)}) copy-start(f32[1,1152,512]{2,1,0:T(8,128)} %param.29) | copy-start | bytes 7077892
  112.5 8.3 %copy-start.13 = (f32[1,1152,512]{2,1,0:T(8,128)S(1)}, f32[1,1152,512]{2,1,0:T(8,128)}, u32[]{:S(2)}) copy-start(f32[1,1152,512]{2,1,0:T(8,128)} %param.28) | copy-start | bytes 7077892
  112.6 8.3 %copy-start.16 = (bf16[512,512]{1,0:T(8,128)(2,1)S(1)}, bf16[512,512]{1,0:T(8,128)(2,1)}, u32[]{:S(2)}) copy-start(bf16[512,512]{1,0:T(8,128)(2,1)} %get-tuple-element.38) | copy-start | bytes 1572868
where the time goes:
time: 129 us; the launch traced here: 128 us
  blocking collectives  41.9 us (32%)
  waiting for transfers between devices  32 us (25%)
  matrix products  23.6 us (18%)
  starting transfers between devices  12.7 us (10%)
  local copies, waits for them, and re-layouts  10.8 us (8%)
  other arithmetic  6.11 us (5%)
    psum x1, blocking collectives, per_device(): centre_total = lax.psum(centre_part, ('group', 'member'))  41.9 us
    all_to_all x1, waiting for transfers between devices, per_device(): lax.all_to_all(packed.reshape(devices, slot_cap, feature_count), ('group'...  28.3 us
    dot_general x1, matrix products, backward_pass(): jnp.dot(latents.T, backward, preferred_element_type=jnp.float32)  8.33 us
    all_to_all x1, starting transfers between devices, per_device(): lax.all_to_all(filled.reshape(devices, slot_cap), ('group', 'member'), sp...  7.33 us
    dot_general x1, matrix products, backward_pass(): jnp.dot(centred.T, preact_grad, preferred_element_type=jnp.float32)  4.83 us
    all_to_all x1, waiting for transfers between devices, per_device(): lax.all_to_all(filled.reshape(devices, slot_cap), ('group', 'member'), sp...  3.7 us
    dot_general x1, matrix products, backward_pass(): jnp.dot(backward, decoder.T, preferred_element_type=jnp.float32) + sparsity  3.69 us
    scatter x1, local copies, waits for them, and re-layouts, per_device(): jnp.zeros((devices * slot_cap, feature_count), jnp.bfloat16).at[position]  3.35 us
  transfers between devices with their start and end apart: 3, of which 2 were waited for; matrix products, arithmetic and copies ran while one was open for 22% of the time, Pallas kernels for 0%

commit v1 on v0

--- a/solution.py
+++ b/solution.py
@@ -11,6 +11,7 @@
 beta_two = 0.999
 adam_eps = 1e-08
 sparsity = 0.1
+EMPTY = 16.0
 
 
 def adam_update(weights_in, gradient, moment_one, moment_two):
@@ -29,7 +30,8 @@
     preact = jnp.dot(centred, encoder, preferred_element_type=jnp.float32) + enc_bias
     positive = jnp.maximum(preact, 0.0)
     latents = (positive * positive).astype(jnp.bfloat16)
-    logits = jnp.dot(in_rows, router_row, preferred_element_type=jnp.float32)
+    router_wide = jnp.broadcast_to(router_row[:, None], (router_row.shape[0], 128))
+    logits = jnp.dot(in_rows, router_wide, preferred_element_type=jnp.float32)[:, 0]
     gating = jax.nn.sigmoid(logits)
     ungated = jnp.dot(latents, decoder, preferred_element_type=jnp.float32)
     rebuilt = centre_bias + gating[:, None] * ungated
@@ -81,38 +83,29 @@
     slot_cap = 2 * row_count // devices
     route_ids = routes[:, 0]
     onehot = (route_ids[:, None] == jnp.arange(devices, dtype=jnp.int32)[None, :]).astype(
-        jnp.float32
-    )
-    earlier = (jnp.arange(row_count)[:, None] > jnp.arange(row_count)[None, :]).astype(jnp.float32)
-    before = jnp.dot(earlier, onehot, precision=lax.Precision.HIGHEST)
-    slot_rank = jnp.sum(before * onehot, axis=1).astype(jnp.int32)
+        jnp.bfloat16
+    )
+    earlier = (jnp.arange(row_count)[:, None] > jnp.arange(row_count)[None, :]).astype(jnp.bfloat16)
+    before = jnp.dot(earlier, onehot, preferred_element_type=jnp.float32)
+    slot_rank = jnp.sum(before * onehot.astype(jnp.float32), axis=1).astype(jnp.int32)
     position = route_ids * slot_cap + slot_rank
-    packed = (
-        jnp.zeros((devices * slot_cap, feature_count), jnp.bfloat16).at[position].set(activations)
-    )
-    filled = (
-        jnp.zeros((devices * slot_cap,), jnp.bfloat16)
-        .at[position]
-        .set(jnp.ones((row_count,), jnp.bfloat16))
-    )
-    arrived, arrived_mask = (
-        lax.all_to_all(
-            packed.reshape(devices, slot_cap, feature_count),
-            ("group", "member"),
-            split_axis=0,
-            concat_axis=0,
-            tiled=True,
-        ),
-        lax.all_to_all(
-            filled.reshape(devices, slot_cap),
-            ("group", "member"),
-            split_axis=0,
-            concat_axis=0,
-            tiled=True,
-        ),
+    chosen = jnp.arange(devices * slot_cap, dtype=jnp.int32)[:, None] == position[None, :]
+    select = chosen.astype(jnp.bfloat16)
+    used = jnp.any(chosen, axis=1)
+    packed = jnp.where(
+        used[:, None],
+        jnp.dot(select, activations, preferred_element_type=jnp.float32),
+        EMPTY,
+    ).astype(jnp.bfloat16)
+    arrived = lax.all_to_all(
+        packed.reshape(devices, slot_cap, feature_count),
+        ("group", "member"),
+        split_axis=0,
+        concat_axis=0,
+        tiled=True,
     )
     in_rows = arrived.reshape(devices * slot_cap, feature_count)
-    live_mask = arrived_mask.reshape(devices * slot_cap).astype(jnp.float32)
+    live_mask = (in_rows[:, 0] < 0.5 * EMPTY).astype(jnp.float32)
     centred, positive, latents, gating, ungated, rebuilt = forward_pass(
         in_rows, centre_bias, router[0], encoder[0], enc_bias[0], decoder[0]
     )
@@ -124,7 +117,12 @@
         concat_axis=0,
         tiled=True,
     )
-    recon = returned.reshape(devices * slot_cap, feature_count)[position]
+    recon = lax.dot_general(
+        select,
+        returned.reshape(devices * slot_cap, feature_count),
+        (((0,), (0,)), ((), ())),
+        preferred_element_type=jnp.float32,
+    ).astype(jnp.bfloat16)
     encoder_grad, bias_grad, decoder_grad, router_grad, centre_part = backward_pass(
         in_rows,
         live_mask,
@@ -141,7 +139,14 @@
     encoder_new = adam_update(encoder[0], encoder_grad, encoder_first[0], encoder_second[0])
     bias_new = adam_update(enc_bias[0], bias_grad, enc_bias_first[0], enc_bias_second[0])
     decoder_new = adam_update(decoder[0], decoder_grad, decoder_first[0], decoder_second[0])
-    centre_total = lax.psum(centre_part, ("group", "member"))
+    centre_all = lax.all_to_all(
+        jnp.broadcast_to(centre_part[None], (devices, feature_count)),
+        ("group", "member"),
+        split_axis=0,
+        concat_axis=0,
+        tiled=True,
+    )
+    centre_total = jnp.sum(centre_all, axis=0)
     centre_new = adam_update(centre_bias, centre_total, centre_first, centre_second)
     return (
         recon,

time: 129 us -> 94.8 us (0.73)
  blocking collectives: 41.9 us -> 0 us
  waiting for transfers between devices: 32 us -> 51.5 us
  local copies, waits for them, and re-layouts: 10.8 us -> 3.24 us
  other arithmetic: 6.11 us -> 2.6 us
    psum x1 -> x0, blocking collectives: 41.9 us -> none  [per_device(): centre_total = lax.psum(centre_part, ('group', 'member'))]
    all_to_all x1, waiting for transfers between devices: 0.01 us -> 13.7 us  [per_device(): lax.all_to_all(outgoing.reshape(devices, slot_cap, feature_count), ('grou...]
    scatter x2 -> x0, local copies, waits for them, and re-layouts: 5.51 us -> none  [the longest x1 3.35 us: per_device(): jnp.zeros((devices * slot_cap, feature_count), jnp.bfloat16).at[position]]
    all_to_all x1, starting transfers between devices: 7.33 us -> 2.58 us  [per_device(): lax.all_to_all(jnp.broadcast_to(centre_part[None], (devices, feature_coun...]
    all_to_all x1, starting transfers between devices: 2.66 us -> 7.33 us  [per_device(): lax.all_to_all(packed.reshape(devices, slot_cap, feature_count), ('group'...]
    all_to_all x1, waiting for transfers between devices: 3.7 us -> 7.83 us  [per_device(): lax.all_to_all(jnp.broadcast_to(centre_part[None], (devices, feature_coun...]
    dot_general x2 -> x4, matrix products: 1.35 us -> 4.3 us  [the longest x1 1.53 us: per_device(): jnp.dot(select, activations, preferred_element_type=jnp.float32)]
    gather x1 -> x0, local copies, waits for them, and re-layouts: 2.2 us -> none  [per_device(): recon = returned.reshape(devices * slot_cap, feature_count)[position]]
  transfers between devices with their start and end apart: 3 -> 3, of which waited for: 2 -> 3; matrix products, arithmetic and copies ran while one was open for 22% -> 18% of each run, Pallas kernels for 0% -> 0%
where the time goes in v1:
time: 94.8 us; the launch traced here: 94.4 us
  waiting for transfers between devices  51.5 us (54%)
  matrix products  23.6 us (25%)
  starting transfers between devices  12.6 us (13%)
  local copies, waits for them, and re-layouts  3.24 us (3%)
  other arithmetic  2.6 us (3%)
    all_to_all x1, waiting for transfers between devices, per_device(): lax.all_to_all(packed.reshape(devices, slot_cap, feature_count), ('group'...  30 us
    all_to_all x1, waiting for transfers between devices, per_device(): lax.all_to_all(outgoing.reshape(devices, slot_cap, feature_count), ('grou...  13.7 us
    dot_general x1, matrix products, backward_pass(): jnp.dot(latents.T, backward, preferred_element_type=jnp.float32)  8.33 us
    all_to_all x1, waiting for transfers between devices, per_device(): lax.all_to_all(jnp.broadcast_to(centre_part[None], (devices, feature_coun...  7.83 us
    all_to_all x1, starting transfers between devices, per_device(): lax.all_to_all(packed.reshape(devices, slot_cap, feature_count), ('group'...  7.33 us
    dot_general x1, matrix products, backward_pass(): jnp.dot(centred.T, preact_grad, preferred_element_type=jnp.float32)  4.8 us
    all_to_all x1, starting transfers between devices, per_device(): lax.all_to_all(outgoing.reshape(devices, slot_cap, feature_count), ('grou...  2.66 us
    all_to_all x1, starting transfers between devices, per_device(): lax.all_to_all(jnp.broadcast_to(centre_part[None], (devices, feature_coun...  2.58 us
  transfers between devices with their start and end apart: 3, of which 3 were waited for; matrix products, arithmetic and copies ran while one was open for 18% of the time, Pallas kernels for 0%

profile of v1, /device:TPU:0, one launch (start us, length us, event | category | flops | bytes accessed | tf_op | source)
XLA Modules:
  0.0 94.4 jit_solution(3830905838166253096)
XLA Ops:
  0.7 1.0 %fusion.23 = f32[256]{0:T(256)S(1)} fusion(s32[256]{0:T(256)} %bitcast.96), kind=kOutput, calls=%fused_computation.39 | convolution fusion | flops 4308736 | bytes 2048 | tf_op jit(solution)/shard_map/dot_general | solution.py:89
  1.6 0.7 convert_add_fusion
  2.5 1.5 %fusion = bf16[512,1152]{1,0:T(8,128)(2,1)} fusion(bf16[256,1152]{1,0:T(8,128)(2,1)S(1)} %copy-done, pred[512]{0:T(512)(128)(4,1)S(1)} %fusion.34, s32[256]{0:T(256)S(1)} %convert_add_fusion), kind=kOutput, calls=%fused_computation.3 | convolution fusion | flops 303300608 | bytes 1771008 | tf_op jit(solution)/shard_map/dot_general | solution.py:97
  4.0 7.3 %all-to-all-start = ((bf16[32,16,1152]{2,1,0:T(8,128)(2,1)}), bf16[32,16,1152]{2,1,0:T(8,128)(2,1)S(1)}, u32[]{:S(2)}, u32[]{:S(2)}) async-start(bf16[32,16,1152]{2,1,0:T(8,128)(2,1)} %bitcast.1), calls=%async_computation | async-start | bytes 2359296 | tf_op jit(solution)/shard_map/all_to_all | solution.py:100
  11.7 30.0 %all-to-all-done = bf16[32,16,1152]{2,1,0:T(8,128)(2,1)S(1)} async-done(((bf16[32,16,1152]{2,1,0:T(8,128)(2,1)}), bf16[32,16,1152]{2,1,0:T(8,128)(2,1)S(1)}, u32[]{:S(2)}, u32[]{:S(2)}) %all-to-all-start) | async-done | bytes 1179680 | tf_op jit(solution)/shard_map/all_to_all | solution.py:100
  41.8 0.4 fusion.52
  42.5 0.8 fusion.9
  43.4 0.4 copy-done.14
  43.7 2.3 %multiply_reduce_fusion = (f32[512]{0:T(512)S(1)}, f32[1152]{0:T(1024)S(1)}, bf16[512,1152]{1,0:T(8,128)(2,1)S(1)}, bf16[512,1152]{1,0:T(8,128)(2,1)}) fusion(f32[512]{0:T(512)S(1)} %convert_reduce_fusion.1, f32[512]{0:T(512)S(1)} %bitcast.90, f32[1152]{0:T(1024)S(1)} %copy-done.3, bf16[32,16,1152]{2,1,0:T(8,128)(2,1)S(1)} %all-to-all-done, ...), kind=kOutput, calls=%fused_computation.15 | convolution fusion | flops 610990464 | bytes 5784576 | tf_op jit(solution)/shard_map/dot_general | solution.py:36
  46.0 1.7 %convert_reduce_fusion = (f32[512]{0:T(512)S(1)}, bf16[512,512]{1,0:T(8,128)(2,1)}) fusion(f32[512]{0:T(512)S(1)} %convert_reduce_fusion.1, f32[512,512]{1,0:T(8,128)S(1)} %fusion.9, bf16[512,1152]{1,0:T(8,128)(2,1)S(1)} %get-tuple-element.33, bf16[1,512,1152]{2,1,0:T(8,128)(2,1)S(1)} %copy-done.14), kind=kOutput, calls=%fused_computation.46 | convolution fusion | flops 605814272 | bytes 3936256 | tf_op jit(solution)/shard_map/dot_general | solution.py:47
  47.8 1.0 %fusion.24 = f32[1152]{0:T(1024)S(1)} fusion(f32[512,1]{0,1:T(1,128)S(1)} %bitcast.91, bf16[1,1152,512]{2,1,0:T(8,128)(2,1)S(1)} %copy-done.1), kind=kOutput, calls=%fused_computation.40 | convolution fusion | flops 7077888 | bytes 1186304 | tf_op jit(solution)/shard_map/dot_general | solution.py:53
  48.8 0.7 broadcast_in_dim.71
  49.6 2.6 %all-to-all-start.2 = ((f32[32,1,1152]{2,1,0:T(1,128)}), f32[32,1,1152]{2,1,0:T(1,128)S(1)}, u32[]{:S(2)}, u32[]{:S(2)}) async-start(f32[32,1,1152]{2,1,0:T(1,128)} %broadcast_in_dim.71), calls=%async_computation.2 | async-start | bytes 294912 | tf_op jit(solution)/shard_map/all_to_all | solution.py:142
  52.2 7.8 %all-to-all-done.2 = f32[32,1,1152]{2,1,0:T(1,128)S(1)} async-done(((f32[32,1,1152]{2,1,0:T(1,128)}), f32[32,1,1152]{2,1,0:T(1,128)S(1)}, u32[]{:S(2)}, u32[]{:S(2)}) %all-to-all-start.2) | async-done | bytes 147488 | tf_op jit(solution)/shard_map/all_to_all | solution.py:142
  60.1 2.7 %all-to-all-start.1 = ((bf16[32,16,1152]{2,1,0:T(8,128)(2,1)}), bf16[32,16,1152]{2,1,0:T(8,128)(2,1)S(1)}, u32[]{:S(2)}, u32[]{:S(2)}) async-start(bf16[32,16,1152]{2,1,0:T(8,128)(2,1)} %bitcast.88), calls=%async_computation.1 | async-start | bytes 2359296 | tf_op jit(solution)/shard_map/all_to_all | solution.py:113
  63.0 0.6 broadcast_in_dim.72
  63.6 0.6 broadcast_in_dim.73
  64.2 0.6 broadcast_in_dim.74
  64.8 0.6 divide_subtract_fusion.1
  65.4 8.3 %fusion.32 = (f32[1,512,1152]{2,1,0:T(8,128)}, bf16[1,512,1152]{2,1,0:T(8,128)(2,1)}, f32[1,512,1152]{2,1,0:T(8,128)}) fusion(f32[1,512,1152]{2,1,0:T(8,128)} %param.33, f32[1,512,1152]{2,1,0:T(8,128)} %param.32, bf16[1,512,1152]{2,1,0:T(8,128)(2,1)} %param.27, bf16[512,1152]{1,0:T(8,128)(2,1)} %copy-done.15, f32[512,512]{1,0:T(8,128)} %copy-done.16), kind=kOutput, calls=%fused_computation.50 | convolution fusion | flops 612761600 | bytes 14024704 | tf_op jit(solution)/shard_map/dot_general | solution.py:46
  73.8 4.8 %fusion.33 = (f32[1,1152,512]{2,1,0:T(8,128)}, bf16[1,1152,512]{2,1,0:T(8,128)(2,1)}, f32[1,1152,512]{2,1,0:T(8,128)}) fusion(f32[1,1152,512]{2,1,0:T(8,128)S(1)} %copy-done.12, f32[1,1152,512]{2,1,0:T(8,128)S(1)} %copy-done.13, bf16[1,1152,512]{2,1,0:T(8,128)(2,1)S(1)} %copy-done.2, bf16[512,512]{1,0:T(8,128)(2,1)S(1)} %copy-done.17, ...), kind=kOutput, calls=%fused_computation.51 | convolution fusion | flops 614006784 | bytes 13505024 | tf_op jit(solution)/shard_map/dot_general | solution.py:49
  78.7 0.6 divide_subtract_fusion
  79.4 13.7 %all-to-all-done.1 = bf16[32,16,1152]{2,1,0:T(8,128)(2,1)S(1)} async-done(((bf16[32,16,1152]{2,1,0:T(8,128)(2,1)}), bf16[32,16,1152]{2,1,0:T(8,128)(2,1)S(1)}, u32[]{:S(2)}, u32[]{:S(2)}) %all-to-all-start.1) | async-done | bytes 1179680 | tf_op jit(solution)/shard_map/all_to_all | solution.py:113
  93.0 1.4 %convolution_convert_fusion = bf16[256,1152]{1,0:T(8,128)(2,1)} fusion(bf16[512,1152]{1,0:T(8,128)(2,1)S(1)} %bitcast.87, s32[256]{0:T(256)S(1)} %convert_add_fusion), kind=kOutput, calls=%fused_computation.6 | convolution fusion | flops 302415872 | bytes 1770496 | tf_op jit(solution)/shard_map/dot_general | solution.py:120
  (46 shorter events, 1.3 us)
Async XLA Ops:
  0.6 1.8 %copy-start = (bf16[256,1152]{1,0:T(8,128)(2,1)S(1)}, bf16[256,1152]{1,0:T(8,128)(2,1)}, u32[]{:S(2)}) copy-start(bf16[256,1152]{1,0:T(8,128)(2,1)} %param.17) | copy-start | bytes 1769476
  2.5 8.9 %copy-start.8 = (bf16[1,1152]{1,0:T(2,128)(2,1)S(1)}, bf16[1,1152]{1,0:T(2,128)(2,1)}, u32[]{:S(2)}) copy-start(bf16[1,1152]{1,0:T(2,128)(2,1)} %param.22) | copy-start | bytes 6916
  4.0 38.2 %copy-start.3 = (f32[1152]{0:T(1024)S(1)}, f32[1152]{0:T(1024)}, u32[]{:S(2)}) copy-start(f32[1152]{0:T(1024)} %param.19) | copy-start | bytes 13828
  4.0 37.6 %all-to-all-start = ((bf16[32,16,1152]{2,1,0:T(8,128)(2,1)}), bf16[32,16,1152]{2,1,0:T(8,128)(2,1)S(1)}, u32[]{:S(2)}, u32[]{:S(2)}) async-start(bf16[32,16,1152]{2,1,0:T(8,128)(2,1)} %bitcast.1), calls=%async_computation | async-start | bytes 2359296 | tf_op jit(solution)/shard_map/all_to_all | solution.py:100
  11.4 31.1 %copy-start.1 = (bf16[1,1152,512]{2,1,0:T(8,128)(2,1)S(1)}, bf16[1,1152,512]{2,1,0:T(8,128)(2,1)}, u32[]{:S(2)}) copy-start(bf16[1,1152,512]{2,1,0:T(8,128)(2,1)} %param.25) | copy-start | bytes 3538948
  11.4 31.1 %copy-start.9 = (f32[1,512]{1,0:T(1,128)S(1)}, f32[1,512]{1,0:T(1,128)}, u32[]{:S(2)}) copy-start(f32[1,512]{1,0:T(1,128)} %param.26) | copy-start | bytes 6148
  42.5 1.3 %copy-start.14 = (bf16[1,512,1152]{2,1,0:T(8,128)(2,1)S(1)}, bf16[1,512,1152]{2,1,0:T(8,128)(2,1)}, u32[]{:S(2)}) copy-start(bf16[1,512,1152]{2,1,0:T(8,128)(2,1)} %param.27) | copy-start | bytes 3538948
  43.3 2.7 %copy-start.16 = (f32[512,512]{1,0:T(8,128)}, f32[512,512]{1,0:T(8,128)S(1)}, u32[]{:S(2)}) copy-start(f32[512,512]{1,0:T(8,128)S(1)} %fusion.9) | copy-start | bytes 3145732
  46.0 1.8 %copy-start.15 = (bf16[512,1152]{1,0:T(8,128)(2,1)}, bf16[512,1152]{1,0:T(8,128)(2,1)S(1)}, u32[]{:S(2)}) copy-start(bf16[512,1152]{1,0:T(8,128)(2,1)S(1)} %get-tuple-element.33) | copy-start | bytes 3538948
  46.0 6.2 %copy-start.6 = (f32[1,1152]{1,0:T(1,128)S(1)}, f32[1,1152]{1,0:T(1,128)}, u32[]{:S(2)}) copy-start(f32[1,1152]{1,0:T(1,128)} %param.24) | copy-start | bytes 13828
  46.0 6.2 %copy-start.7 = (f32[1,1152]{1,0:T(1,128)S(1)}, f32[1,1152]{1,0:T(1,128)}, u32[]{:S(2)}) copy-start(f32[1,1152]{1,0:T(1,128)} %param.23) | copy-start | bytes 13828
  48.8 16.0 %copy-start.10 = (f32[1,512]{1,0:T(1,128)S(1)}, f32[1,512]{1,0:T(1,128)}, u32[]{:S(2)}) copy-start(f32[1,512]{1,0:T(1,128)} %param.30) | copy-start | bytes 6148
  48.8 16.0 %copy-start.11 = (f32[1,512]{1,0:T(1,128)S(1)}, f32[1,512]{1,0:T(1,128)}, u32[]{:S(2)}) copy-start(f32[1,512]{1,0:T(1,128)} %param.31) | copy-start | bytes 6148
  49.6 10.5 %all-to-all-start.2 = ((f32[32,1,1152]{2,1,0:T(1,128)}), f32[32,1,1152]{2,1,0:T(1,128)S(1)}, u32[]{:S(2)}, u32[]{:S(2)}) async-start(f32[32,1,1152]{2,1,0:T(1,128)} %broadcast_in_dim.71), calls=%async_computation.2 | async-start | bytes 294912 | tf_op jit(solution)/shard_map/all_to_all | solution.py:142
  60.1 33.0 %all-to-all-start.1 = ((bf16[32,16,1152]{2,1,0:T(8,128)(2,1)}), bf16[32,16,1152]{2,1,0:T(8,128)(2,1)S(1)}, u32[]{:S(2)}, u32[]{:S(2)}) async-start(bf16[32,16,1152]{2,1,0:T(8,128)(2,1)} %bitcast.88), calls=%async_computation.1 | async-start | bytes 2359296 | tf_op jit(solution)/shard_map/all_to_all | solution.py:113
  65.4 8.3 %copy-start.2 = (bf16[1,1152,512]{2,1,0:T(8,128)(2,1)S(1)}, bf16[1,1152,512]{2,1,0:T(8,128)(2,1)}, u32[]{:S(2)}) copy-start(bf16[1,1152,512]{2,1,0:T(8,128)(2,1)} %param.25) | copy-start | bytes 3538948
  65.4 8.3 %copy-start.12 = (f32[1,1152,512]{2,1,0:T(8,128)S(1)}, f32[1,1152,512]{2,1,0:T(8,128)}, u32[]{:S(2)}) copy-start(f32[1,1152,512]{2,1,0:T(8,128)} %param.29) | copy-start | bytes 7077892
  65.4 8.3 %copy-start.13 = (f32[1,1152,512]{2,1,0:T(8,128)S(1)}, f32[1,1152,512]{2,1,0:T(8,128)}, u32[]{:S(2)}) copy-start(f32[1,1152,512]{2,1,0:T(8,128)} %param.28) | copy-start | bytes 7077892
  65.4 8.3 %copy-start.17 = (bf16[512,512]{1,0:T(8,128)(2,1)S(1)}, bf16[512,512]{1,0:T(8,128)(2,1)}, u32[]{:S(2)}) copy-start(bf16[512,512]{1,0:T(8,128)(2,1)} %get-tuple-element.38) | copy-start | bytes 1572868
  73.8 4.9 %copy-start.4 = (f32[1152]{0:T(1024)S(1)}, f32[1152]{0:T(1024)}, u32[]{:S(2)}) copy-start(f32[1152]{0:T(1024)} %param.20) | copy-start | bytes 13828
  73.8 4.9 %copy-start.5 = (f32[1152]{0:T(1024)S(1)}, f32[1152]{0:T(1024)}, u32[]{:S(2)}) copy-start(f32[1152]{0:T(1024)} %param.21) | copy-start | bytes 13828

commit v2 on v1

--- a/solution.py
+++ b/solution.py
@@ -1,7 +1,13 @@
+import functools
+
 import jax
 import jax.numpy as jnp
 from jax import lax
+from jax.experimental import pallas as pl
+from jax.experimental.pallas import tpu as pltpu
 from jax.sharding import PartitionSpec as P
+
+MESH = pl.DeviceIdType.MESH
 
 STEP = 10
 
@@ -54,6 +60,197 @@
         encoder.astype(jnp.float32), bias_grad, precision=lax.Precision.HIGHEST
     )
     return (encoder_grad, bias_grad, decoder_grad, router_grad, centre_part)
+
+
+def flipped(index, bits):
+    result, place = index, 1
+    while place <= bits:
+        if bits & place:
+            result = result + (1 - 2 * lax.rem(lax.div(index, place), 2)) * place
+        place *= 2
+    return result
+
+
+def partner_of(offset, members):
+    return (
+        flipped(lax.axis_index("group"), offset // members),
+        flipped(lax.axis_index("member"), offset % members),
+    )
+
+
+def greet(devices, members):
+    barrier = pltpu.get_barrier_semaphore()
+    for offset in range(1, devices):
+        pl.semaphore_signal(
+            barrier, inc=1, device_id=partner_of(offset, members), device_id_type=MESH
+        )
+    pl.semaphore_wait(barrier, devices - 1)
+
+
+def dispatch_order(devices, members):
+    half = members // 2
+    near = [offset for offset in range(devices) if not offset & half]
+    return near + [offset + half for offset in near]
+
+
+def dispatch_kernel(
+    devices,
+    members,
+    packed_ref,
+    centre_ref,
+    router_ref,
+    encoder_ref,
+    bias_ref,
+    decoder_ref,
+    rows_ref,
+    outgoing_ref,
+    positive_ref,
+    ungated_ref,
+    gating_ref,
+    encoder_buf,
+    decoder_buf,
+    local_sem,
+    send_sem,
+    recv_sem,
+):
+    me = lax.axis_index("group") * members + lax.axis_index("member")
+    slot_cap = packed_ref.shape[1]
+    order = dispatch_order(devices, members)
+    greet(devices, members)
+    copies = [None] * devices
+    half = devices // 2
+    for step in range(devices):
+        place = step // 2 if step % 2 else half + step // 2
+        if order[place] == 0:
+            continue
+        group, member = partner_of(order[place], members)
+        copies[place] = pltpu.make_async_remote_copy(
+            src_ref=packed_ref.at[group * members + member],
+            dst_ref=rows_ref.at[place],
+            send_sem=send_sem.at[place],
+            recv_sem=recv_sem.at[place],
+            device_id=(group, member),
+            device_id_type=MESH,
+        )
+        copies[place].start()
+    own = pltpu.make_async_copy(packed_ref.at[me], rows_ref.at[0], local_sem.at[0])
+    first = pltpu.make_async_copy(encoder_ref, encoder_buf, local_sem.at[1])
+    second = pltpu.make_async_copy(decoder_ref, decoder_buf, local_sem.at[2])
+    own.start()
+    first.start()
+    second.start()
+    own.wait()
+    first.wait()
+    second.wait()
+    per_chunk = max(1, 128 // slot_cap)
+    centre = centre_ref[...]
+    router = router_ref[...].astype(jnp.float32)
+    for start in range(0, devices, per_chunk):
+        places = range(start, min(start + per_chunk, devices))
+        for place in places:
+            if copies[place] is not None:
+                copies[place].wait_recv()
+        amount = len(places) * slot_cap
+        chunk = pl.ds(start * slot_cap, amount)
+        rows = rows_ref[pl.ds(start, len(places))].reshape(amount, rows_ref.shape[2])
+        wide = rows.astype(jnp.float32)
+        gating = jax.nn.sigmoid(jnp.sum(wide * router, axis=1, keepdims=True))
+        centred = (wide - centre).astype(jnp.bfloat16)
+        preact = (
+            jnp.dot(centred, encoder_buf[...], preferred_element_type=jnp.float32) + bias_ref[...]
+        )
+        positive = jnp.maximum(preact, 0.0)
+        latents = (positive * positive).astype(jnp.bfloat16)
+        ungated = jnp.dot(latents, decoder_buf[...], preferred_element_type=jnp.float32)
+        rebuilt = (centre + gating * ungated).astype(jnp.bfloat16)
+        for number, place in enumerate(places):
+            group, member = partner_of(order[place], members)
+            outgoing_ref[group * members + member] = rebuilt[
+                number * slot_cap : (number + 1) * slot_cap
+            ]
+        positive_ref[chunk] = positive
+        ungated_ref[chunk] = ungated
+        gating_ref[chunk] = jnp.broadcast_to(gating, (amount, gating_ref.shape[1]))
+    for copy in copies:
+        if copy is not None:
+            copy.wait_send()
+
+
+def dispatch_and_forward(packed, centre_bias, router_row, encoder, enc_bias, decoder, members):
+    devices, slot_cap, features = packed.shape
+    latent_count = encoder.shape[1]
+    slots = devices * slot_cap
+    in_vmem = pl.BlockSpec(memory_space=pltpu.VMEM)
+    anywhere = pl.BlockSpec(memory_space=pl.ANY)
+    return pl.pallas_call(
+        functools.partial(dispatch_kernel, devices, members),
+        out_shape=(
+            jax.ShapeDtypeStruct((devices, slot_cap, features), jnp.bfloat16),
+            jax.ShapeDtypeStruct((devices, slot_cap, features), jnp.bfloat16),
+            jax.ShapeDtypeStruct((slots, latent_count), jnp.float32),
+            jax.ShapeDtypeStruct((slots, features), jnp.float32),
+            jax.ShapeDtypeStruct((slots, 128), jnp.float32),
+        ),
+        in_specs=[anywhere, in_vmem, in_vmem, anywhere, in_vmem, anywhere],
+        out_specs=(in_vmem,) * 5,
+        scratch_shapes=[
+            pltpu.VMEM(encoder.shape, encoder.dtype),
+            pltpu.VMEM(decoder.shape, decoder.dtype),
+            pltpu.SemaphoreType.DMA((3,)),
+            pltpu.SemaphoreType.DMA((devices,)),
+            pltpu.SemaphoreType.DMA((devices,)),
+        ],
+        compiler_params=pltpu.CompilerParams(
+            collective_id=0, has_side_effects=True, vmem_limit_bytes=32 << 20
+        ),
+        name="dispatch_forward",
+    )(packed, centre_bias[None], router_row[None], encoder, enc_bias[None], decoder)
+
+
+def centre_kernel(devices, members, part_ref, total_ref, parts, send_sem, recv_sem):
+    greet(devices, members)
+    copies = []
+    for offset in range(1, devices):
+        copies.append(
+            pltpu.make_async_remote_copy(
+                src_ref=part_ref,
+                dst_ref=parts.at[lax.axis_index("group") * members + lax.axis_index("member")],
+                send_sem=send_sem.at[offset],
+                recv_sem=recv_sem.at[offset],
+                device_id=partner_of(offset, members),
+                device_id_type=MESH,
+            )
+        )
+        copies[-1].start()
+    parts[lax.axis_index("group") * members + lax.axis_index("member")] = part_ref[...]
+    for copy in copies:
+        copy.wait_recv()
+    total_ref[...] = jnp.sum(parts[...], axis=0)
+    for copy in copies:
+        copy.wait_send()
+
+
+def centre_sum(part, devices, members):
+    shape = (1, part.shape[0])
+    return pl.pallas_call(
+        functools.partial(centre_kernel, devices, members),
+        out_shape=jax.ShapeDtypeStruct(shape, jnp.float32),
+        in_specs=[pl.BlockSpec(memory_space=pltpu.VMEM)],
+        out_specs=pl.BlockSpec(memory_space=pltpu.VMEM),
+        scratch_shapes=[
+            pltpu.VMEM((devices,) + shape, jnp.float32),
+            pltpu.SemaphoreType.DMA((devices,)),
+            pltpu.SemaphoreType.DMA((devices,)),
+        ],
+        compiler_params=pltpu.CompilerParams(
+            collective_id=1, has_side_effects=True, vmem_limit_bytes=4 << 20
+        ),
+        name="centre_sum",
+    )(part[None])[0]
+
+
+def power_of_two(number):
+    return number & (number - 1) == 0
 
 
 def per_device(
@@ -97,19 +294,27 @@
         jnp.dot(select, activations, preferred_element_type=jnp.float32),
         EMPTY,
     ).astype(jnp.bfloat16)
-    arrived = lax.all_to_all(
-        packed.reshape(devices, slot_cap, feature_count),
-        ("group", "member"),
-        split_axis=0,
-        concat_axis=0,
-        tiled=True,
-    )
-    in_rows = arrived.reshape(devices * slot_cap, feature_count)
+    packed = packed.reshape(devices, slot_cap, feature_count)
+    aligned = slot_cap % 16 == 0 and power_of_two(groups) and power_of_two(members)
+    if aligned and members > 1:
+        arrived, outgoing, positive, ungated, gating_wide = dispatch_and_forward(
+            packed, centre_bias, router[0], encoder[0], enc_bias[0], decoder[0], members
+        )
+        in_rows = arrived.reshape(devices * slot_cap, feature_count)
+        gating = gating_wide[:, 0]
+        centred = (in_rows.astype(jnp.float32) - centre_bias).astype(jnp.bfloat16)
+        latents = (positive * positive).astype(jnp.bfloat16)
+        rebuilt = centre_bias + gating[:, None] * ungated
+    else:
+        arrived = lax.all_to_all(
+            packed, ("group", "member"), split_axis=0, concat_axis=0, tiled=True
+        )
+        in_rows = arrived.reshape(devices * slot_cap, feature_count)
+        centred, positive, latents, gating, ungated, rebuilt = forward_pass(
+            in_rows, centre_bias, router[0], encoder[0], enc_bias[0], decoder[0]
+        )
+        outgoing = rebuilt.astype(jnp.bfloat16)
     live_mask = (in_rows[:, 0] < 0.5 * EMPTY).astype(jnp.float32)
-    centred, positive, latents, gating, ungated, rebuilt = forward_pass(
-        in_rows, centre_bias, router[0], encoder[0], enc_bias[0], decoder[0]
-    )
-    outgoing = rebuilt.astype(jnp.bfloat16)
     returned = lax.all_to_all(
         outgoing.reshape(devices, slot_cap, feature_count),
         ("group", "member"),
@@ -139,14 +344,10 @@
     encoder_new = adam_update(encoder[0], encoder_grad, encoder_first[0], encoder_second[0])
     bias_new = adam_update(enc_bias[0], bias_grad, enc_bias_first[0], enc_bias_second[0])
     decoder_new = adam_update(decoder[0], decoder_grad, decoder_first[0], decoder_second[0])
-    centre_all = lax.all_to_all(
-        jnp.broadcast_to(centre_part[None], (devices, feature_count)),
-        ("group", "member"),
-        split_axis=0,
-        concat_axis=0,
-        tiled=True,
-    )
-    centre_total = jnp.sum(centre_all, axis=0)
+    if power_of_two(groups) and power_of_two(members):
+        centre_total = centre_sum(centre_part, devices, members)
+    else:
+        centre_total = lax.psum(centre_part, ("group", "member"))
     centre_new = adam_update(centre_bias, centre_total, centre_first, centre_second)
     return (
         recon,

time: 94.8 us -> 97.7 us (1.031)
  Pallas kernels: 0 us -> 56.7 us
  waiting for transfers between devices: 51.5 us -> 0.01 us
  starting transfers between devices: 12.6 us -> 4.98 us
  other arithmetic: 2.6 us -> 6.24 us
  local copies, waits for them, and re-layouts: 3.24 us -> 6.16 us
  matrix products: 23.6 us -> 22.3 us
    pallas_call x0 -> x2, Pallas kernels: none -> 56.7 us  [the longest x1 33.7 us: dispatch_and_forward(): pl.pallas_call(functools.partial(dispatch_kernel, devices, members), out_...]
    all_to_all x2 -> x0, waiting for transfers between devices: 37.8 us -> none  [the longest x1 30 us: per_device(): lax.all_to_all(packed.reshape(devices, slot_cap, feature_count), ('group'...]
    all_to_all x1, waiting for transfers between devices: 13.7 us -> 0.01 us  [per_device(): lax.all_to_all(outgoing.reshape(devices, slot_cap, feature_count), ('grou...]
    all_to_all x2 -> x0, starting transfers between devices: 9.9 us -> none  [the longest x1 7.33 us: per_device(): lax.all_to_all(packed.reshape(devices, slot_cap, feature_count), ('group'...]
    dot_general x3 -> x0, matrix products: 3.54 us -> none  [the longest x1 2.25 us: forward_pass(): ungated = jnp.dot(latents, decoder, preferred_element_type=jnp.float32)]
    reduce_sum x1, other arithmetic: 0.1 us -> 3.58 us  [backward_pass(): jnp.sum(errors * ungated, axis=1)]
    unnamed x36, local copies, waits for them, and re-layouts: 0.49 us -> 3.5 us
    all_to_all x1, starting transfers between devices: 2.66 us -> 4.98 us  [per_device(): lax.all_to_all(outgoing.reshape(devices, slot_cap, feature_count), ('grou...]
  transfers between devices with their start and end apart: 3 -> 1, of which waited for: 3 -> 0; matrix products, arithmetic and copies ran while one was open for 18% -> 26% of each run, Pallas kernels for 0% -> 24%
where the time goes in v2:
time: 97.7 us; the launch traced here: 97.3 us
  Pallas kernels  56.7 us (58%)
  matrix products  22.3 us (23%)
  other arithmetic  6.24 us (6%)
  local copies, waits for them, and re-layouts  6.16 us (6%)
  starting transfers between devices  4.98 us (5%)
    pallas_call x1, Pallas kernels, dispatch_and_forward(): pl.pallas_call(functools.partial(dispatch_kernel, devices, members), out_...  33.7 us
    pallas_call x1, Pallas kernels, centre_sum(): pl.pallas_call(functools.partial(centre_kernel, devices, members), out_sh...  22.9 us
    dot_general x1, matrix products, backward_pass(): jnp.dot(latents.T, backward, preferred_element_type=jnp.float32)  8.32 us
    all_to_all x1, starting transfers between devices, per_device(): lax.all_to_all(outgoing.reshape(devices, slot_cap, feature_count), ('grou...  4.98 us
    dot_general x1, matrix products, backward_pass(): jnp.dot(centred.T, preact_grad, preferred_element_type=jnp.float32)  4.81 us
    dot_general x1, matrix products, backward_pass(): jnp.dot(backward, decoder.T, preferred_element_type=jnp.float32) + sparsity  3.68 us
    reduce_sum x1, other arithmetic, backward_pass(): jnp.sum(errors * ungated, axis=1)  3.58 us
    unnamed x36, local copies, waits for them, and re-layouts  3.5 us
  transfers between devices with their start and end apart: 1, of which 0 were waited for; matrix products, arithmetic and copies ran while one was open for 26% of the time, Pallas kernels for 24%

profile of v2, /device:TPU:0, one launch (start us, length us, event | category | flops | bytes accessed | tf_op | source)
XLA Modules:
  0.0 97.3 jit_solution(12685155412910140356)
XLA Ops:
  0.7 1.0 %fusion.15 = f32[256]{0:T(256)S(1)} fusion(s32[256]{0:T(256)} %bitcast.73), kind=kOutput, calls=%fused_computation.28 | convolution fusion | flops 4308736 | bytes 2048 | tf_op jit(solution)/shard_map/dot_general | solution.py:286
  1.8 0.7 convert_add_fusion
  2.4 0.2 fusion.21
  2.6 0.7 broadcast_in_dim.60.centre_ref
  3.3 0.5 fusion
  3.9 33.7 %dispatch_forward.1 = (bf16[32,16,1152]{2,1,0:T(8,128)(2,1)S(1)}, bf16[32,16,1152]{2,1,0:T(8,128)(2,1)S(1)}, f32[512,512]{1,0:T(8,128)S(1)}, f32[512,1152]{1,0:T(8,128)S(1)}, f32[512,128]{1,0:T(8,128)S(1)}) custom-call(bf16[32,16,1152]{2,1,0:T(8,128)(2,1)S(1)} %bitcast.69, f32[1,1152]{1,0:T(1,128)S(1)} %broadcast_in_dim.60.centre_ref, ...), custom_call_target="tpu_custom_call" | custom-call | tf_op jit(solution)/shard_map/dispatch_forward/pallas_call | solution.py:185
  37.7 1.4 %copy-done.2 = f32[512,1152]{1,0:T(8,128)} copy-done((f32[512,1152]{1,0:T(8,128)}, f32[512,1152]{1,0:T(8,128)S(1)}, u32[]{:S(2)}) %copy-start.2) | copy-done | bytes 2359320
  39.1 1.0 %copy-done.4 = bf16[32,16,1152]{2,1,0:T(8,128)(2,1)} copy-done((bf16[32,16,1152]{2,1,0:T(8,128)(2,1)}, bf16[32,16,1152]{2,1,0:T(8,128)(2,1)S(1)}, u32[]{:S(2)}) %copy-start.4) | copy-done | bytes 1179672
  40.1 1.0 copy-done.7
  41.1 5.0 %all-to-all-start = ((bf16[32,16,1152]{2,1,0:T(8,128)(2,1)}), bf16[32,16,1152]{2,1,0:T(8,128)(2,1)}, u32[]{:S(2)}, u32[]{:S(2)}) async-start(bf16[32,16,1152]{2,1,0:T(8,128)(2,1)} %copy-done.4), calls=%async_computation | async-start | bytes 2359296 | tf_op jit(solution)/shard_map/all_to_all | solution.py:318
  46.2 0.2 slice_reduce_fusion
  46.5 3.6 %multiply_reduce_fusion = (f32[512]{0:T(512)S(1)}, f32[1152]{0:T(1024)S(1)}, bf16[512,1152]{1,0:T(8,128)(2,1)}) fusion(f32[512,1152]{1,0:T(8,128)} %copy-done.2, f32[512]{0:T(512)S(1)} %convert_reduce_fusion.1, f32[512]{0:T(512)S(1)} %get-tuple-element.28, f32[1152]{0:T(1024)S(1)} %copy-done.8, bf16[32,16,1152]{2,1,0:T(8,128)(2,1)S(1)} %get-tuple-element.22, ...), kind=kLoop, calls=%fused_computation.15 | loop fusion | flops 5896576 | bytes 4736000 | tf_op jit(solution)/shard_map/reduce_sum | solution.py:57
  50.4 0.3 convolution_reduce_fusion
  50.7 3.7 %convert_reduce_fusion = (f32[512]{0:T(512)S(1)}, bf16[512,512]{1,0:T(8,128)(2,1)}) fusion(f32[512]{0:T(512)S(1)} %convert_reduce_fusion.1, f32[512,512]{1,0:T(8,128)} %copy-done.7, bf16[512,1152]{1,0:T(8,128)(2,1)} %get-tuple-element.45, bf16[1,512,1152]{2,1,0:T(8,128)(2,1)} %param.27), kind=kOutput, calls=%fused_computation.32 | convolution fusion | flops 605814272 | bytes 3936256 | tf_op jit(solution)/shard_map/dot_general | solution.py:53
  54.4 1.0 %convolution_reduce_fusion.1 = f32[1152]{0:T(1024)S(1)} fusion(f32[512,1]{0,1:T(1,128)S(1)} %bitcast.70, bf16[1,1152,512]{2,1,0:T(8,128)(2,1)S(1)} %copy-done.1), kind=kOutput, calls=%fused_computation.30 | convolution fusion | flops 7077888 | bytes 1186304 | tf_op jit(solution)/shard_map/dot_general | solution.py:59
  55.5 0.6 broadcast_in_dim.62
  56.1 0.6 broadcast_in_dim.63
  56.7 0.6 broadcast_in_dim.64
  57.3 22.9 %centre_sum.1 = f32[1,1152]{1,0:T(1,128)S(1)} custom-call(f32[1,1152]{1,0:T(1,128)S(1)} %broadcast_in_dim.61.part_ref), custom_call_target="tpu_custom_call" | custom-call | tf_op jit(solution)/shard_map/centre_sum/pallas_call | solution.py:235
  80.3 0.6 divide_subtract_fusion.1
  80.9 0.6 divide_subtract_fusion
  81.5 8.3 %fusion.18 = (f32[1,512,1152]{2,1,0:T(8,128)}, bf16[1,512,1152]{2,1,0:T(8,128)(2,1)}, f32[1,512,1152]{2,1,0:T(8,128)}) fusion(f32[1,512,1152]{2,1,0:T(8,128)} %param.33, f32[1,512,1152]{2,1,0:T(8,128)} %param.32, bf16[1,512,1152]{2,1,0:T(8,128)(2,1)} %param.27, bf16[512,1152]{1,0:T(8,128)(2,1)} %get-tuple-element.45, f32[512,512]{1,0:T(8,128)} %copy-done.7), kind=kOutput, calls=%fused_computation.35 | convolution fusion | flops 612761600 | bytes 14024704 | tf_op jit(solution)/shard_map/dot_general | solution.py:52
  89.8 4.8 %fusion.19 = (f32[1,1152,512]{2,1,0:T(8,128)}, bf16[1,1152,512]{2,1,0:T(8,128)(2,1)}, f32[1,1152,512]{2,1,0:T(8,128)}) fusion(f32[1,1152,512]{2,1,0:T(8,128)S(1)} %copy-done.15, f32[1,1152,512]{2,1,0:T(8,128)S(1)} %copy-done.16, bf16[1,1152,512]{2,1,0:T(8,128)(2,1)S(1)} %copy-done.1, bf16[512,512]{1,0:T(8,128)(2,1)S(1)} %copy-done.17, ...), kind=kOutput, calls=%fused_computation.36 | convolution fusion | flops 614006784 | bytes 13505024 | tf_op jit(solution)/shard_map/dot_general | solution.py:55
  94.7 2.6 %convolution_convert_fusion = bf16[256,1152]{1,0:T(8,128)(2,1)} fusion(bf16[512,1152]{1,0:T(8,128)(2,1)} %bitcast.4, s32[256]{0:T(256)S(1)} %convert_add_fusion), kind=kOutput, calls=%fused_computation.6 | convolution fusion | flops 302415872 | bytes 1770496 | tf_op jit(solution)/shard_map/dot_general | solution.py:325
  (45 shorter events, 0.6 us)
Async XLA Ops:
  0.6 2.7 %copy-start = (bf16[256,1152]{1,0:T(8,128)(2,1)S(1)}, bf16[256,1152]{1,0:T(8,128)(2,1)}, u32[]{:S(2)}) copy-start(bf16[256,1152]{1,0:T(8,128)(2,1)} %param.17) | copy-start | bytes 1769476
  0.7 3.2 %copy-start.6 = (f32[1,512]{1,0:T(1,128)S(1)}, f32[1,512]{1,0:T(1,128)}, u32[]{:S(2)}) copy-start(f32[1,512]{1,0:T(1,128)} %bias_ref.1) | copy-start | bytes 6148
  0.7 3.2 %copy-start.5 = (bf16[1,1152]{1,0:T(2,128)(2,1)S(1)}, bf16[1,1152]{1,0:T(2,128)(2,1)}, u32[]{:S(2)}) copy-start(bf16[1,1152]{1,0:T(2,128)(2,1)} %router_ref.1) | copy-start | bytes 6916
  0.7 3.2 %copy-start.1 = (bf16[1,1152,512]{2,1,0:T(8,128)(2,1)S(1)}, bf16[1,1152,512]{2,1,0:T(8,128)(2,1)}, u32[]{:S(2)}) copy-start(bf16[1,1152,512]{2,1,0:T(8,128)(2,1)} %param.25) | copy-start | bytes 3538948
  0.7 3.2 %copy-start.3 = (bf16[1,512,1152]{2,1,0:T(8,128)(2,1)S(1)}, bf16[1,512,1152]{2,1,0:T(8,128)(2,1)}, u32[]{:S(2)}) copy-start(bf16[1,512,1152]{2,1,0:T(8,128)(2,1)} %param.27) | copy-start | bytes 3538948
  3.9 42.5 %copy-start.8 = (f32[1152]{0:T(1024)S(1)}, f32[1152]{0:T(1024)}, u32[]{:S(2)}) copy-start(f32[1152]{0:T(1024)} %param.19) | copy-start | bytes 13828
  37.6 1.4 %copy-start.2 = (f32[512,1152]{1,0:T(8,128)}, f32[512,1152]{1,0:T(8,128)S(1)}, u32[]{:S(2)}) copy-start(f32[512,1152]{1,0:T(8,128)S(1)} %get-tuple-element.24) | copy-start | bytes 7077892
  39.0 1.0 %copy-start.4 = (bf16[32,16,1152]{2,1,0:T(8,128)(2,1)}, bf16[32,16,1152]{2,1,0:T(8,128)(2,1)S(1)}, u32[]{:S(2)}) copy-start(bf16[32,16,1152]{2,1,0:T(8,128)(2,1)S(1)} %get-tuple-element.21) | copy-start | bytes 3538948
  40.1 1.0 copy-start.7
  41.1 53.6 %all-to-all-start = ((bf16[32,16,1152]{2,1,0:T(8,128)(2,1)}), bf16[32,16,1152]{2,1,0:T(8,128)(2,1)}, u32[]{:S(2)}, u32[]{:S(2)}) async-start(bf16[32,16,1152]{2,1,0:T(8,128)(2,1)} %copy-done.4), calls=%async_computation | async-start | bytes 2359296 | tf_op jit(solution)/shard_map/all_to_all | solution.py:318
  46.4 4.2 %copy-start.11 = (f32[1,1152]{1,0:T(1,128)S(1)}, f32[1,1152]{1,0:T(1,128)}, u32[]{:S(2)}) copy-start(f32[1,1152]{1,0:T(1,128)} %param.24) | copy-start | bytes 13828
  46.4 4.2 %copy-start.12 = (f32[1,1152]{1,0:T(1,128)S(1)}, f32[1,1152]{1,0:T(1,128)}, u32[]{:S(2)}) copy-start(f32[1,1152]{1,0:T(1,128)} %param.23) | copy-start | bytes 13828
  50.7 29.6 %copy-start.13 = (f32[1,512]{1,0:T(1,128)S(1)}, f32[1,512]{1,0:T(1,128)}, u32[]{:S(2)}) copy-start(f32[1,512]{1,0:T(1,128)} %param.30) | copy-start | bytes 6148
  50.7 29.6 %copy-start.14 = (f32[1,512]{1,0:T(1,128)S(1)}, f32[1,512]{1,0:T(1,128)}, u32[]{:S(2)}) copy-start(f32[1,512]{1,0:T(1,128)} %param.31) | copy-start | bytes 6148
  50.7 30.2 %copy-start.9 = (f32[1152]{0:T(1024)S(1)}, f32[1152]{0:T(1024)}, u32[]{:S(2)}) copy-start(f32[1152]{0:T(1024)} %param.20) | copy-start | bytes 13828
  50.7 30.1 %copy-start.10 = (f32[1152]{0:T(1024)S(1)}, f32[1152]{0:T(1024)}, u32[]{:S(2)}) copy-start(f32[1152]{0:T(1024)} %param.21) | copy-start | bytes 13828
  81.5 8.3 %copy-start.15 = (f32[1,1152,512]{2,1,0:T(8,128)S(1)}, f32[1,1152,512]{2,1,0:T(8,128)}, u32[]{:S(2)}) copy-start(f32[1,1152,512]{2,1,0:T(8,128)} %param.29) | copy-start | bytes 7077892
  81.5 8.3 %copy-start.16 = (f32[1,1152,512]{2,1,0:T(8,128)S(1)}, f32[1,1152,512]{2,1,0:T(8,128)}, u32[]{:S(2)}) copy-start(f32[1,1152,512]{2,1,0:T(8,128)} %param.28) | copy-start | bytes 7077892
  81.5 8.3 %copy-start.17 = (bf16[512,512]{1,0:T(8,128)(2,1)S(1)}, bf16[512,512]{1,0:T(8,128)(2,1)}, u32[]{:S(2)}) copy-start(bf16[512,512]{1,0:T(8,128)(2,1)} %get-tuple-element.47) | copy-start | bytes 1572868

commit v3 on v2

--- a/solution.py
+++ b/solution.py
@@ -93,6 +93,17 @@
     return near + [offset + half for offset in near]
 
 
+def three_parts(values):
+    high = values.astype(jnp.bfloat16).astype(jnp.float32)
+    middle = (values - high).astype(jnp.bfloat16).astype(jnp.float32)
+    low = values - high - middle
+    row = lax.broadcasted_iota(jnp.int32, (16, values.shape[1]), 0)
+    stacked = jnp.where(
+        row == 0, high, jnp.where(row == 1, middle, jnp.where(row == 2, low, 0.0))
+    )
+    return stacked.astype(jnp.bfloat16)
+
+
 def dispatch_kernel(
     devices,
     members,
@@ -102,19 +113,31 @@
     encoder_ref,
     bias_ref,
     decoder_ref,
-    rows_ref,
     outgoing_ref,
-    positive_ref,
-    ungated_ref,
-    gating_ref,
+    centred_ref,
+    latents_ref,
+    backward_ref,
+    preact_grad_ref,
+    centre_part_ref,
+    bias_grad_ref,
+    router_grad_ref,
     encoder_buf,
     decoder_buf,
+    rows_buf,
+    outgoing_buf,
+    centred_buf,
+    latents_buf,
+    backward_buf,
+    preact_grad_buf,
     local_sem,
+    out_sem,
+    save_sem,
     send_sem,
     recv_sem,
 ):
     me = lax.axis_index("group") * members + lax.axis_index("member")
     slot_cap = packed_ref.shape[1]
+    features = packed_ref.shape[2]
     order = dispatch_order(devices, members)
     greet(devices, members)
     copies = [None] * devices
@@ -126,14 +149,14 @@
         group, member = partner_of(order[place], members)
         copies[place] = pltpu.make_async_remote_copy(
             src_ref=packed_ref.at[group * members + member],
-            dst_ref=rows_ref.at[place],
+            dst_ref=rows_buf.at[place],
             send_sem=send_sem.at[place],
             recv_sem=recv_sem.at[place],
             device_id=(group, member),
             device_id_type=MESH,
         )
         copies[place].start()
-    own = pltpu.make_async_copy(packed_ref.at[me], rows_ref.at[0], local_sem.at[0])
+    own = pltpu.make_async_copy(packed_ref.at[me], rows_buf.at[0], local_sem.at[0])
     first = pltpu.make_async_copy(encoder_ref, encoder_buf, local_sem.at[1])
     second = pltpu.make_async_copy(decoder_ref, decoder_buf, local_sem.at[2])
     own.start()
@@ -145,6 +168,10 @@
     per_chunk = max(1, 128 // slot_cap)
     centre = centre_ref[...]
     router = router_ref[...].astype(jnp.float32)
+    error_sum = jnp.zeros((1, features), jnp.float32)
+    router_grad = jnp.zeros((1, features), jnp.float32)
+    bias_grad = jnp.zeros(bias_ref.shape, jnp.float32)
+    saves = []
     for start in range(0, devices, per_chunk):
         places = range(start, min(start + per_chunk, devices))
         for place in places:
@@ -152,8 +179,8 @@
                 copies[place].wait_recv()
         amount = len(places) * slot_cap
         chunk = pl.ds(start * slot_cap, amount)
-        rows = rows_ref[pl.ds(start, len(places))].reshape(amount, rows_ref.shape[2])
-        wide = rows.astype(jnp.float32)
+        wide = rows_buf[pl.ds(start, len(places))].reshape(amount, features).astype(jnp.float32)
+        live = (wide[:, :1] < 0.5 * EMPTY).astype(jnp.float32)
         gating = jax.nn.sigmoid(jnp.sum(wide * router, axis=1, keepdims=True))
         centred = (wide - centre).astype(jnp.bfloat16)
         preact = (
@@ -162,48 +189,109 @@
         positive = jnp.maximum(preact, 0.0)
         latents = (positive * positive).astype(jnp.bfloat16)
         ungated = jnp.dot(latents, decoder_buf[...], preferred_element_type=jnp.float32)
-        rebuilt = (centre + gating * ungated).astype(jnp.bfloat16)
-        for number, place in enumerate(places):
+        rebuilt = centre + gating * ungated
+        outgoing_buf[pl.ds(start, len(places))] = rebuilt.astype(jnp.bfloat16).reshape(
+            len(places), slot_cap, features
+        )
+        for place in places:
             group, member = partner_of(order[place], members)
-            outgoing_ref[group * members + member] = rebuilt[
-                number * slot_cap : (number + 1) * slot_cap
-            ]
-        positive_ref[chunk] = positive
-        ungated_ref[chunk] = ungated
-        gating_ref[chunk] = jnp.broadcast_to(gating, (amount, gating_ref.shape[1]))
+            saves.append(
+                pltpu.make_async_copy(
+                    outgoing_buf.at[place],
+                    outgoing_ref.at[group * members + member],
+                    out_sem.at[place],
+                )
+            )
+            saves[-1].start()
+        errors = (wide - rebuilt) * live
+        backward = (-gating * errors).astype(jnp.bfloat16)
+        latent_grad = (
+            lax.dot_general(
+                backward,
+                decoder_buf[...],
+                (((1,), (1,)), ((), ())),
+                preferred_element_type=jnp.float32,
+            )
+            + sparsity
+        )
+        preact_grad = (latent_grad * 2.0 * positive * live).astype(jnp.bfloat16)
+        logit_grad = -jnp.sum(errors * ungated, axis=1, keepdims=True) * gating * (1.0 - gating)
+        logit_grad = logit_grad.astype(jnp.bfloat16).astype(jnp.float32)
+        error_sum = error_sum + jnp.sum(errors, axis=0, keepdims=True)
+        router_grad = router_grad + jnp.sum(logit_grad * wide, axis=0, keepdims=True)
+        bias_grad = bias_grad + jnp.sum(preact_grad.astype(jnp.float32), axis=0, keepdims=True)
+        for number, (value, buf, ref) in enumerate(
+            (
+                (centred, centred_buf, centred_ref),
+                (latents, latents_buf, latents_ref),
+                (backward, backward_buf, backward_ref),
+                (preact_grad, preact_grad_buf, preact_grad_ref),
+            )
+        ):
+            buf[chunk] = value
+            saves.append(
+                pltpu.make_async_copy(
+                    buf.at[chunk], ref.at[chunk], save_sem.at[start // per_chunk, number]
+                )
+            )
+            saves[-1].start()
+    bias_grad_ref[...] = bias_grad
+    router_grad_ref[...] = router_grad
+    products = lax.dot_general(
+        three_parts(bias_grad),
+        encoder_buf[...],
+        (((1,), (1,)), ((), ())),
+        preferred_element_type=jnp.float32,
+    )
+    centre_part_ref[...] = -error_sum - jnp.sum(products, axis=0, keepdims=True)
+    for save in saves:
+        save.wait()
     for copy in copies:
         if copy is not None:
             copy.wait_send()
 
 
-def dispatch_and_forward(packed, centre_bias, router_row, encoder, enc_bias, decoder, members):
+def dispatch_and_compute(packed, centre_bias, router_row, encoder, enc_bias, decoder, members):
     devices, slot_cap, features = packed.shape
     latent_count = encoder.shape[1]
     slots = devices * slot_cap
+    chunks = -(-devices // max(1, 128 // slot_cap))
     in_vmem = pl.BlockSpec(memory_space=pltpu.VMEM)
     anywhere = pl.BlockSpec(memory_space=pl.ANY)
+    wide, narrow = (slots, features), (slots, latent_count)
     return pl.pallas_call(
         functools.partial(dispatch_kernel, devices, members),
         out_shape=(
-            jax.ShapeDtypeStruct((devices, slot_cap, features), jnp.bfloat16),
-            jax.ShapeDtypeStruct((devices, slot_cap, features), jnp.bfloat16),
-            jax.ShapeDtypeStruct((slots, latent_count), jnp.float32),
-            jax.ShapeDtypeStruct((slots, features), jnp.float32),
-            jax.ShapeDtypeStruct((slots, 128), jnp.float32),
+            jax.ShapeDtypeStruct(packed.shape, jnp.bfloat16),
+            jax.ShapeDtypeStruct(wide, jnp.bfloat16),
+            jax.ShapeDtypeStruct(narrow, jnp.bfloat16),
+            jax.ShapeDtypeStruct(wide, jnp.bfloat16),
+            jax.ShapeDtypeStruct(narrow, jnp.bfloat16),
+            jax.ShapeDtypeStruct((1, features), jnp.float32),
+            jax.ShapeDtypeStruct((1, latent_count), jnp.float32),
+            jax.ShapeDtypeStruct((1, features), jnp.float32),
         ),
         in_specs=[anywhere, in_vmem, in_vmem, anywhere, in_vmem, anywhere],
-        out_specs=(in_vmem,) * 5,
+        out_specs=(anywhere,) * 5 + (in_vmem,) * 3,
         scratch_shapes=[
             pltpu.VMEM(encoder.shape, encoder.dtype),
             pltpu.VMEM(decoder.shape, decoder.dtype),
+            pltpu.VMEM(packed.shape, jnp.bfloat16),
+            pltpu.VMEM(packed.shape, jnp.bfloat16),
+            pltpu.VMEM(wide, jnp.bfloat16),
+            pltpu.VMEM(narrow, jnp.bfloat16),
+            pltpu.VMEM(wide, jnp.bfloat16),
+            pltpu.VMEM(narrow, jnp.bfloat16),
             pltpu.SemaphoreType.DMA((3,)),
+            pltpu.SemaphoreType.DMA((devices,)),
+            pltpu.SemaphoreType.DMA((chunks, 4)),
             pltpu.SemaphoreType.DMA((devices,)),
             pltpu.SemaphoreType.DMA((devices,)),
         ],
         compiler_params=pltpu.CompilerParams(
-            collective_id=0, has_side_effects=True, vmem_limit_bytes=32 << 20
+            collective_id=0, has_side_effects=True, vmem_limit_bytes=61 << 20
         ),
-        name="dispatch_forward",
+        name="dispatch_compute",
     )(packed, centre_bias[None], router_row[None], encoder, enc_bias[None], decoder)
 
 
@@ -296,25 +384,24 @@
     ).astype(jnp.bfloat16)
     packed = packed.reshape(devices, slot_cap, feature_count)
     aligned = slot_cap % 16 == 0 and power_of_two(groups) and power_of_two(members)
-    if aligned and members > 1:
-        arrived, outgoing, positive, ungated, gating_wide = dispatch_and_forward(
-            packed, centre_bias, router[0], encoder[0], enc_bias[0], decoder[0], members
-        )
-        in_rows = arrived.reshape(devices * slot_cap, feature_count)
-        gating = gating_wide[:, 0]
-        centred = (in_rows.astype(jnp.float32) - centre_bias).astype(jnp.bfloat16)
-        latents = (positive * positive).astype(jnp.bfloat16)
-        rebuilt = centre_bias + gating[:, None] * ungated
+    aligned = aligned and members > 1
+    if aligned:
+        outgoing, centred, latents, backward, preact_grad, centre_part, bias_grad, router_grad = (
+            dispatch_and_compute(
+                packed, centre_bias, router[0], encoder[0], enc_bias[0], decoder[0], members
+            )
+        )
+        centre_part, bias_grad, router_grad = centre_part[0], bias_grad[0], router_grad[0]
     else:
         arrived = lax.all_to_all(
             packed, ("group", "member"), split_axis=0, concat_axis=0, tiled=True
         )
         in_rows = arrived.reshape(devices * slot_cap, feature_count)
+        live_mask = (in_rows[:, 0] < 0.5 * EMPTY).astype(jnp.float32)
         centred, positive, latents, gating, ungated, rebuilt = forward_pass(
             in_rows, centre_bias, router[0], encoder[0], enc_bias[0], decoder[0]
         )
         outgoing = rebuilt.astype(jnp.bfloat16)
-    live_mask = (in_rows[:, 0] < 0.5 * EMPTY).astype(jnp.float32)
     returned = lax.all_to_all(
         outgoing.reshape(devices, slot_cap, feature_count),
         ("group", "member"),
@@ -328,23 +415,32 @@
         (((0,), (0,)), ((), ())),
         preferred_element_type=jnp.float32,
     ).astype(jnp.bfloat16)
-    encoder_grad, bias_grad, decoder_grad, router_grad, centre_part = backward_pass(
-        in_rows,
-        live_mask,
-        centred,
-        positive,
-        latents,
-        gating,
-        ungated,
-        rebuilt,
-        encoder[0],
-        decoder[0],
-    )
+    if aligned:
+        decoder_grad = jnp.dot(latents.T, backward, preferred_element_type=jnp.float32)
+        encoder_grad = jnp.dot(centred.T, preact_grad, preferred_element_type=jnp.float32)
+    else:
+        encoder_grad, bias_grad, decoder_grad, router_grad, centre_part = backward_pass(
+            in_rows,
+            live_mask,
+            centred,
+            positive,
+            latents,
+            gating,
+            ungated,
+            rebuilt,
+            encoder[0],
+            decoder[0],
+        )
     router_new = adam_update(router[0], router_grad, router_first[0], router_second[0])
     encoder_new = adam_update(encoder[0], encoder_grad, encoder_first[0], encoder_second[0])
     bias_new = adam_update(enc_bias[0], bias_grad, enc_bias_first[0], enc_bias_second[0])
     decoder_new = adam_update(decoder[0], decoder_grad, decoder_first[0], decoder_second[0])
     if power_of_two(groups) and power_of_two(members):
+        centre_part, first, second = lax.optimization_barrier(
+            (centre_part, encoder_new[1], decoder_new[1])
+        )
+        encoder_new = (encoder_new[0], first, encoder_new[2])
+        decoder_new = (decoder_new[0], second, decoder_new[2])
         centre_total = centre_sum(centre_part, devices, members)
     else:
         centre_total = lax.psum(centre_part, ("group", "member"))

time: 97.7 us -> 84.9 us (0.87)
  matrix products: 22.3 us -> 16.5 us
  local copies, waits for them, and re-layouts: 6.16 us -> 1.41 us
  other arithmetic: 6.24 us -> 2.76 us
  Pallas kernels: 56.7 us -> 58.3 us
    dot_general x5 -> x2, matrix products: 18.1 us -> 12.6 us  [the longest x1 7.88 us: per_device(): jnp.dot(latents.T, backward, preferred_element_type=jnp.float32)]
    reduce_sum x1 -> x0, other arithmetic: 3.58 us -> none  [backward_pass(): jnp.sum(errors * ungated, axis=1)]
    unnamed x36 -> x38, local copies, waits for them, and re-layouts: 3.5 us -> 0.11 us
    pallas_call x1, Pallas kernels: 33.7 us -> 36.7 us  [dispatch_and_compute(): pl.pallas_call(functools.partial(dispatch_kernel, devices, members), out_...]
    pallas_call x1, Pallas kernels: 22.9 us -> 21.5 us  [centre_sum(): pl.pallas_call(functools.partial(centre_kernel, devices, members), out_sh...]
    dot_general x1, matrix products: 2.64 us -> 1.37 us  [per_device(): lax.dot_general(select, returned.reshape(devices * slot_cap, feature_coun...]
    broadcast_in_dim x4 -> x1, local copies, waits for them, and re-layouts: 2.49 us -> 1.3 us  [dispatch_and_compute(): centre_bias[None]]
    dot_general x1, matrix products: 0.52 us -> 1.53 us  [per_device(): jnp.dot(select, activations, preferred_element_type=jnp.float32)]
  transfers between devices with their start and end apart: 1 -> 1, of which waited for: 0 -> 0; matrix products, arithmetic and copies ran while one was open for 26% -> 17% of each run, Pallas kernels for 24% -> 25%
where the time goes in v3:
time: 84.9 us; the launch traced here: 84.6 us
  Pallas kernels  58.3 us (69%)
  matrix products  16.5 us (19%)
  starting transfers between devices  4.71 us (6%)
  other arithmetic  2.76 us (3%)
  local copies, waits for them, and re-layouts  1.41 us (2%)
  between operations  0.91 us (1%)
    pallas_call x1, Pallas kernels, dispatch_and_compute(): pl.pallas_call(functools.partial(dispatch_kernel, devices, members), out_...  36.7 us
    pallas_call x1, Pallas kernels, centre_sum(): pl.pallas_call(functools.partial(centre_kernel, devices, members), out_sh...  21.5 us
    dot_general x1, matrix products, per_device(): jnp.dot(latents.T, backward, preferred_element_type=jnp.float32)  7.88 us
    dot_general x1, matrix products, per_device(): jnp.dot(centred.T, preact_grad, preferred_element_type=jnp.float32)  4.75 us
    all_to_all x1, starting transfers between devices, per_device(): lax.all_to_all(outgoing.reshape(devices, slot_cap, feature_count), ('grou...  4.71 us
  transfers between devices with their start and end apart: 1, of which 0 were waited for; matrix products, arithmetic and copies ran while one was open for 17% of the time, Pallas kernels for 25%

profile of v3, /device:TPU:0, one launch (start us, length us, event | category | flops | bytes accessed | tf_op | source)
XLA Modules:
  0.0 84.6 jit_solution(11687821164166017694)
XLA Ops:
  0.6 0.0 copy-start
  0.7 1.0 %fusion.5 = f32[256]{0:T(256)S(1)} fusion(s32[256]{0:T(256)} %bitcast.47), kind=kOutput, calls=%fused_computation.14 | convolution fusion | flops 4308736 | bytes 2048 | tf_op jit(solution)/shard_map/dot_general | solution.py:374
  1.6 0.7 convert_add_fusion
  2.3 0.2 fusion.8
  2.5 1.3 %broadcast_in_dim.50.centre_ref = f32[1,1152]{1,0:T(1,128)} reshape(f32[1152]{0:T(1024)} %param.19) | data formatting | bytes 9216 | tf_op jit(solution)/shard_map/broadcast_in_dim | solution.py:295
  3.8 1.5 %fusion = bf16[512,1152]{1,0:T(8,128)(2,1)} fusion(bf16[256,1152]{1,0:T(8,128)(2,1)S(1)} %copy-done, pred[512]{0:T(512)(128)(4,1)S(1)} %fusion.8, s32[256]{0:T(256)S(1)} %convert_add_fusion), kind=kOutput, calls=%fused_computation.3 | convolution fusion | flops 303300608 | bytes 1771008 | tf_op jit(solution)/shard_map/dot_general | solution.py:382
  5.3 36.7 %dispatch_compute.1 = (bf16[32,16,1152]{2,1,0:T(8,128)(2,1)}, bf16[512,1152]{1,0:T(8,128)(2,1)}, bf16[512,512]{1,0:T(8,128)(2,1)}, bf16[512,1152]{1,0:T(8,128)(2...) custom-call(bf16[32,16,1152]{2,1,0:T(8,128)(2,1)} %bitcast.46, ...), custom_call_target="tpu_custom_call" | custom-call | tf_op jit(solution)/shard_map/dispatch_compute/pallas_call | solution.py:262
  42.1 4.7 %all-to-all-start = ((bf16[32,16,1152]{2,1,0:T(8,128)(2,1)}), bf16[32,16,1152]{2,1,0:T(8,128)(2,1)S(1)}, u32[]{:S(2)}, u32[]{:S(2)}) async-start(bf16[32,16,1152]{2,1,0:T(8,128)(2,1)} %get-tuple-element.27), calls=%async_computation | async-start | bytes 2359296 | tf_op jit(solution)/shard_map/all_to_all | solution.py:405
  46.8 0.0 copy-start.2
  46.8 0.0 copy-start.15
  46.9 0.0 copy-start.16
  46.9 7.9 %fusion.6 = (f32[1,512,1152]{2,1,0:T(8,128)}, bf16[1,512,1152]{2,1,0:T(8,128)(2,1)}, f32[512,1152]{1,0:T(8,128)}) fusion(f32[1,512,1152]{2,1,0:T(8,128)} %param.33, f32[1,512,1152]{2,1,0:T(8,128)} %param.32, bf16[1,512,1152]{2,1,0:T(8,128)(2,1)S(1)} %copy-done.1, bf16[512,512]{1,0:T(8,128)(2,1)} %get-tuple-element.31, bf16[512,1152]{1,0:T(8,128)(2,1)} %get-tuple-element.32), kind=kOutput, calls=%fused_computation.15 | convolution fusion | flops 612237312 | bytes 13500416 | tf_op jit(solution)/shard_map/dot_general | solution.py:419
  54.8 0.0 copy-start.5
  54.8 0.0 copy-start.12
  54.8 0.0 copy-start.3
  54.9 0.0 copy-start.6
  54.9 0.0 copy-start.9
  54.9 0.0 copy-start.10
  54.9 4.8 %fusion.7 = (f32[1,1152,512]{2,1,0:T(8,128)}, bf16[1,1152,512]{2,1,0:T(8,128)(2,1)}, f32[1152,512]{1,0:T(8,128)}) fusion(f32[1,1152,512]{2,1,0:T(8,128)S(1)} %copy-done.15, f32[1,1152,512]{2,1,0:T(8,128)S(1)} %copy-done.16, bf16[1,1152,512]{2,1,0:T(8,128)(2,1)S(1)} %copy-done.2, bf16[512,1152]{1,0:T(8,128)(2,1)S(1)} %copy-done.17, ...), kind=kOutput, calls=%fused_computation.16 | convolution fusion | flops 612237312 | bytes 13500416 | tf_op jit(solution)/shard_map/dot_general | solution.py:420
  59.7 21.5 %centre_sum.1 = f32[1,1152]{1,0:T(1,128)S(1)} custom-call(f32[1,1152]{1,0:T(1,128)S(1)} %broadcast_in_dim.51.part_ref), custom_call_target="tpu_custom_call" | custom-call | tf_op jit(solution)/shard_map/centre_sum/pallas_call | solution.py:323
  81.3 0.6 divide_subtract_fusion.1
  81.9 0.6 divide_subtract_fusion
  82.6 0.6 subtract_convert_fusion.2
  83.2 1.4 %convolution_convert_fusion = bf16[256,1152]{1,0:T(8,128)(2,1)} fusion(bf16[512,1152]{1,0:T(8,128)(2,1)S(1)} %bitcast.43, s32[256]{0:T(256)S(1)} %convert_add_fusion), kind=kOutput, calls=%fused_computation.4 | convolution fusion | flops 302415872 | bytes 1770496 | tf_op jit(solution)/shard_map/dot_general | solution.py:412
  (32 shorter events, 0.1 us)
Async XLA Ops:
  0.6 3.1 %copy-start = (bf16[256,1152]{1,0:T(8,128)(2,1)S(1)}, bf16[256,1152]{1,0:T(8,128)(2,1)}, u32[]{:S(2)}) copy-start(bf16[256,1152]{1,0:T(8,128)(2,1)} %param.17) | copy-start | bytes 1769476
  5.3 41.5 %copy-start.1 = (bf16[1,512,1152]{2,1,0:T(8,128)(2,1)S(1)}, bf16[1,512,1152]{2,1,0:T(8,128)(2,1)}, u32[]{:S(2)}) copy-start(bf16[1,512,1152]{2,1,0:T(8,128)(2,1)} %param.27) | copy-start | bytes 3538948
  42.1 4.7 %copy-start.8 = (f32[1,1152]{1,0:T(1,128)S(1)}, f32[1,1152]{1,0:T(1,128)}, u32[]{:S(2)}) copy-start(f32[1,1152]{1,0:T(1,128)} %get-tuple-element.28) | copy-start | bytes 13828
  42.1 41.1 %all-to-all-start = ((bf16[32,16,1152]{2,1,0:T(8,128)(2,1)}), bf16[32,16,1152]{2,1,0:T(8,128)(2,1)S(1)}, u32[]{:S(2)}, u32[]{:S(2)}) async-start(bf16[32,16,1152]{2,1,0:T(8,128)(2,1)} %get-tuple-element.27), calls=%async_computation | async-start | bytes 2359296 | tf_op jit(solution)/shard_map/all_to_all | solution.py:405
  46.8 7.9 %copy-start.2 = (bf16[1,1152,512]{2,1,0:T(8,128)(2,1)S(1)}, bf16[1,1152,512]{2,1,0:T(8,128)(2,1)}, u32[]{:S(2)}) copy-start(bf16[1,1152,512]{2,1,0:T(8,128)(2,1)} %param.25) | copy-start | bytes 3538948
  46.8 7.9 %copy-start.15 = (f32[1,1152,512]{2,1,0:T(8,128)S(1)}, f32[1,1152,512]{2,1,0:T(8,128)}, u32[]{:S(2)}) copy-start(f32[1,1152,512]{2,1,0:T(8,128)} %param.29) | copy-start | bytes 7077892
  46.9 7.9 %copy-start.16 = (f32[1,1152,512]{2,1,0:T(8,128)S(1)}, f32[1,1152,512]{2,1,0:T(8,128)}, u32[]{:S(2)}) copy-start(f32[1,1152,512]{2,1,0:T(8,128)} %param.28) | copy-start | bytes 7077892
  46.9 7.9 %copy-start.17 = (bf16[512,1152]{1,0:T(8,128)(2,1)S(1)}, bf16[512,1152]{1,0:T(8,128)(2,1)}, u32[]{:S(2)}) copy-start(bf16[512,1152]{1,0:T(8,128)(2,1)} %get-tuple-element.29) | copy-start | bytes 3538948
  46.9 7.9 %copy-start.18 = (bf16[512,512]{1,0:T(8,128)(2,1)S(1)}, bf16[512,512]{1,0:T(8,128)(2,1)}, u32[]{:S(2)}) copy-start(bf16[512,512]{1,0:T(8,128)(2,1)} %get-tuple-element.30) | copy-start | bytes 1572868
  54.8 26.5 %copy-start.5 = (f32[1,512]{1,0:T(1,128)S(1)}, f32[1,512]{1,0:T(1,128)}, u32[]{:S(2)}) copy-start(f32[1,512]{1,0:T(1,128)} %bias_ref.1) | copy-start | bytes 6148
  54.8 26.5 %copy-start.12 = (f32[1,512]{1,0:T(1,128)S(1)}, f32[1,512]{1,0:T(1,128)}, u32[]{:S(2)}) copy-start(f32[1,512]{1,0:T(1,128)} %param.30) | copy-start | bytes 6148
  54.8 26.5 %copy-start.13 = (f32[1,512]{1,0:T(1,128)S(1)}, f32[1,512]{1,0:T(1,128)}, u32[]{:S(2)}) copy-start(f32[1,512]{1,0:T(1,128)} %param.31) | copy-start | bytes 6148
  54.8 26.5 %copy-start.14 = (f32[1,512]{1,0:T(1,128)S(1)}, f32[1,512]{1,0:T(1,128)}, u32[]{:S(2)}) copy-start(f32[1,512]{1,0:T(1,128)} %get-tuple-element.35) | copy-start | bytes 6148
  54.8 27.1 %copy-start.3 = (f32[1152]{0:T(1024)S(1)}, f32[1152]{0:T(1024)}, u32[]{:S(2)}) copy-start(f32[1152]{0:T(1024)} %param.19) | copy-start | bytes 13828
  54.9 27.1 %copy-start.6 = (f32[1152]{0:T(1024)S(1)}, f32[1152]{0:T(1024)}, u32[]{:S(2)}) copy-start(f32[1152]{0:T(1024)} %param.20) | copy-start | bytes 13828
  54.9 27.1 %copy-start.7 = (f32[1152]{0:T(1024)S(1)}, f32[1152]{0:T(1024)}, u32[]{:S(2)}) copy-start(f32[1152]{0:T(1024)} %param.21) | copy-start | bytes 13828
  54.9 27.7 %copy-start.4 = (bf16[1,1152]{1,0:T(2,128)(2,1)S(1)}, bf16[1,1152]{1,0:T(2,128)(2,1)}, u32[]{:S(2)}) copy-start(bf16[1,1152]{1,0:T(2,128)(2,1)} %router_ref.1) | copy-start | bytes 6916
  54.9 27.7 %copy-start.9 = (f32[1,1152]{1,0:T(1,128)S(1)}, f32[1,1152]{1,0:T(1,128)}, u32[]{:S(2)}) copy-start(f32[1,1152]{1,0:T(1,128)} %param.23) | copy-start | bytes 13828
  54.9 27.6 %copy-start.10 = (f32[1,1152]{1,0:T(1,128)S(1)}, f32[1,1152]{1,0:T(1,128)}, u32[]{:S(2)}) copy-start(f32[1,1152]{1,0:T(1,128)} %param.24) | copy-start | bytes 13828
  54.9 27.6 %copy-start.11 = (f32[1,1152]{1,0:T(1,128)S(1)}, f32[1,1152]{1,0:T(1,128)}, u32[]{:S(2)}) copy-start(f32[1,1152]{1,0:T(1,128)} %get-tuple-element.34) | copy-start | bytes 13828

commit v4 on v3

--- a/solution.py
+++ b/solution.py
@@ -118,7 +118,7 @@
     latents_ref,
     backward_ref,
     preact_grad_ref,
-    centre_part_ref,
+    centre_total_ref,
     bias_grad_ref,
     router_grad_ref,
     encoder_buf,
@@ -134,6 +134,10 @@
     save_sem,
     send_sem,
     recv_sem,
+    part_buf,
+    parts_buf,
+    part_send_sem,
+    part_recv_sem,
 ):
     me = lax.axis_index("group") * members + lax.axis_index("member")
     slot_cap = packed_ref.shape[1]
@@ -243,12 +247,32 @@
         (((1,), (1,)), ((), ())),
         preferred_element_type=jnp.float32,
     )
-    centre_part_ref[...] = -error_sum - jnp.sum(products, axis=0, keepdims=True)
+    part = -error_sum - jnp.sum(products, axis=0, keepdims=True)
+    part_buf[...] = part
+    part_copies = []
+    for offset in range(1, devices):
+        part_copies.append(
+            pltpu.make_async_remote_copy(
+                src_ref=part_buf,
+                dst_ref=parts_buf.at[me],
+                send_sem=part_send_sem.at[offset],
+                recv_sem=part_recv_sem.at[offset],
+                device_id=partner_of(offset, members),
+                device_id_type=MESH,
+            )
+        )
+        part_copies[-1].start()
+    parts_buf[me] = part
     for save in saves:
         save.wait()
     for copy in copies:
         if copy is not None:
             copy.wait_send()
+    for copy in part_copies:
+        copy.wait_recv()
+    centre_total_ref[...] = jnp.sum(parts_buf[...], axis=0)
+    for copy in part_copies:
+        copy.wait_send()
 
 
 def dispatch_and_compute(packed, centre_bias, router_row, encoder, enc_bias, decoder, members):
@@ -287,54 +311,16 @@
             pltpu.SemaphoreType.DMA((chunks, 4)),
             pltpu.SemaphoreType.DMA((devices,)),
             pltpu.SemaphoreType.DMA((devices,)),
+            pltpu.VMEM((1, features), jnp.float32),
+            pltpu.VMEM((devices, 1, features), jnp.float32),
+            pltpu.SemaphoreType.DMA((devices,)),
+            pltpu.SemaphoreType.DMA((devices,)),
         ],
         compiler_params=pltpu.CompilerParams(
             collective_id=0, has_side_effects=True, vmem_limit_bytes=61 << 20
         ),
         name="dispatch_compute",
     )(packed, centre_bias[None], router_row[None], encoder, enc_bias[None], decoder)
-
-
-def centre_kernel(devices, members, part_ref, total_ref, parts, send_sem, recv_sem):
-    greet(devices, members)
-    copies = []
-    for offset in range(1, devices):
-        copies.append(
-            pltpu.make_async_remote_copy(
-                src_ref=part_ref,
-                dst_ref=parts.at[lax.axis_index("group") * members + lax.axis_index("member")],
-                send_sem=send_sem.at[offset],
-                recv_sem=recv_sem.at[offset],
-                device_id=partner_of(offset, members),
-                device_id_type=MESH,
-            )
-        )
-        copies[-1].start()
-    parts[lax.axis_index("group") * members + lax.axis_index("member")] = part_ref[...]
-    for copy in copies:
-        copy.wait_recv()
-    total_ref[...] = jnp.sum(parts[...], axis=0)
-    for copy in copies:
-        copy.wait_send()
-
-
-def centre_sum(part, devices, members):
-    shape = (1, part.shape[0])
-    return pl.pallas_call(
-        functools.partial(centre_kernel, devices, members),
-        out_shape=jax.ShapeDtypeStruct(shape, jnp.float32),
-        in_specs=[pl.BlockSpec(memory_space=pltpu.VMEM)],
-        out_specs=pl.BlockSpec(memory_space=pltpu.VMEM),
-        scratch_shapes=[
-            pltpu.VMEM((devices,) + shape, jnp.float32),
-            pltpu.SemaphoreType.DMA((devices,)),
-            pltpu.SemaphoreType.DMA((devices,)),
-        ],
-        compiler_params=pltpu.CompilerParams(
-            collective_id=1, has_side_effects=True, vmem_limit_bytes=4 << 20
-        ),
-        name="centre_sum",
-    )(part[None])[0]
 
 
 def power_of_two(number):
@@ -386,12 +372,12 @@
     aligned = slot_cap % 16 == 0 and power_of_two(groups) and power_of_two(members)
     aligned = aligned and members > 1
     if aligned:
-        outgoing, centred, latents, backward, preact_grad, centre_part, bias_grad, router_grad = (
+        outgoing, centred, latents, backward, preact_grad, centre_total, bias_grad, router_grad = (
             dispatch_and_compute(
                 packed, centre_bias, router[0], encoder[0], enc_bias[0], decoder[0], members
             )
         )
-        centre_part, bias_grad, router_grad = centre_part[0], bias_grad[0], router_grad[0]
+        centre_total, bias_grad, router_grad = centre_total[0], bias_grad[0], router_grad[0]
     else:
         arrived = lax.all_to_all(
             packed, ("group", "member"), split_axis=0, concat_axis=0, tiled=True
@@ -435,14 +421,7 @@
     encoder_new = adam_update(encoder[0], encoder_grad, encoder_first[0], encoder_second[0])
     bias_new = adam_update(enc_bias[0], bias_grad, enc_bias_first[0], enc_bias_second[0])
     decoder_new = adam_update(decoder[0], decoder_grad, decoder_first[0], decoder_second[0])
-    if power_of_two(groups) and power_of_two(members):
-        centre_part, first, second = lax.optimization_barrier(
-            (centre_part, encoder_new[1], decoder_new[1])
-        )
-        encoder_new = (encoder_new[0], first, encoder_new[2])
-        decoder_new = (decoder_new[0], second, decoder_new[2])
-        centre_total = centre_sum(centre_part, devices, members)
-    else:
+    if not aligned:
         centre_total = lax.psum(centre_part, ("group", "member"))
     centre_new = adam_update(centre_bias, centre_total, centre_first, centre_second)
     return (

time: 84.9 us -> 85.6 us (level)
  waiting for transfers between devices: 0.01 us -> 15.6 us
  Pallas kernels: 58.3 us -> 45.4 us
  starting transfers between devices: 4.71 us -> 2.67 us
    pallas_call x1 -> x0, Pallas kernels: 21.5 us -> none  [centre_sum(): pl.pallas_call(functools.partial(centre_kernel, devices, members), out_sh...]
    all_to_all x1, waiting for transfers between devices: 0.01 us -> 15.6 us  [per_device(): lax.all_to_all(outgoing.reshape(devices, slot_cap, feature_count), ('grou...]
    pallas_call x1, Pallas kernels: 36.7 us -> 45.4 us  [dispatch_and_compute(): pl.pallas_call(functools.partial(dispatch_kernel, devices, members), out_...]
    all_to_all x1, starting transfers between devices: 4.71 us -> 2.67 us  [per_device(): lax.all_to_all(outgoing.reshape(devices, slot_cap, feature_count), ('grou...]
  transfers between devices with their start and end apart: 1 -> 1, of which waited for: 0 -> 1; matrix products, arithmetic and copies ran while one was open for 17% -> 17% of each run, Pallas kernels for 25% -> 0%
where the time goes in v4:
time: 85.6 us; the launch traced here: 85.2 us
  Pallas kernels  45.4 us (53%)
  matrix products  16.5 us (19%)
  waiting for transfers between devices  15.6 us (18%)
  other arithmetic  2.73 us (3%)
  starting transfers between devices  2.67 us (3%)
  local copies, waits for them, and re-layouts  1.39 us (2%)
  between operations  0.87 us (1%)
    pallas_call x1, Pallas kernels, dispatch_and_compute(): pl.pallas_call(functools.partial(dispatch_kernel, devices, members), out_...  45.4 us
    all_to_all x1, waiting for transfers between devices, per_device(): lax.all_to_all(outgoing.reshape(devices, slot_cap, feature_count), ('grou...  15.6 us
    dot_general x1, matrix products, per_device(): jnp.dot(latents.T, backward, preferred_element_type=jnp.float32)  7.9 us
    dot_general x1, matrix products, per_device(): jnp.dot(centred.T, preact_grad, preferred_element_type=jnp.float32)  4.76 us
    all_to_all x1, starting transfers between devices, per_device(): lax.all_to_all(outgoing.reshape(devices, slot_cap, feature_count), ('grou...  2.67 us
  transfers between devices with their start and end apart: 1, of which 1 were waited for; matrix products, arithmetic and copies ran while one was open for 17% of the time, Pallas kernels for 0%

profile of v4, /device:TPU:0, one launch (start us, length us, event | category | flops | bytes accessed | tf_op | source)
XLA Modules:
  0.0 85.2 jit_solution(14437901128766856638)
XLA Ops:
  0.6 0.0 copy-start
  0.7 1.0 %fusion.5 = f32[256]{0:T(256)S(1)} fusion(s32[256]{0:T(256)} %bitcast.53), kind=kOutput, calls=%fused_computation.14 | convolution fusion | flops 4308736 | bytes 2048 | tf_op jit(solution)/shard_map/dot_general | solution.py:360
  1.6 0.7 convert_add_fusion
  2.3 0.2 fusion.10
  2.5 1.3 %broadcast_in_dim.47.centre_ref = f32[1,1152]{1,0:T(1,128)} reshape(f32[1152]{0:T(1024)} %param.19) | data formatting | bytes 9216 | tf_op jit(solution)/shard_map/broadcast_in_dim | solution.py:323
  3.8 1.5 %fusion = bf16[512,1152]{1,0:T(8,128)(2,1)} fusion(bf16[256,1152]{1,0:T(8,128)(2,1)S(1)} %copy-done, pred[512]{0:T(512)(128)(4,1)S(1)} %fusion.10, s32[256]{0:T(256)S(1)} %convert_add_fusion), kind=kOutput, calls=%fused_computation.3 | convolution fusion | flops 303300608 | bytes 1771008 | tf_op jit(solution)/shard_map/dot_general | solution.py:368
  5.3 0.0 copy-start.6
  5.3 0.0 copy-start.7
  5.3 0.0 copy-start.4
  5.4 0.0 copy-start.9
  5.4 0.0 copy-start.10
  5.4 0.0 copy-start.1
  5.4 45.4 %dispatch_compute.1 = (bf16[32,16,1152]{2,1,0:T(8,128)(2,1)}, bf16[512,1152]{1,0:T(8,128)(2,1)}, bf16[512,512]{1,0:T(8,128)(2,1)}, bf16[512,1152]{1,0:T(8,128)(2...) custom-call(bf16[32,16,1152]{2,1,0:T(8,128)(2,1)} %bitcast.52, ...), custom_call_target="tpu_custom_call" | custom-call | tf_op jit(solution)/shard_map/dispatch_compute/pallas_call | solution.py:286
  50.9 2.7 %all-to-all-start = ((bf16[32,16,1152]{2,1,0:T(8,128)(2,1)}), bf16[32,16,1152]{2,1,0:T(8,128)(2,1)S(1)}, u32[]{:S(2)}, u32[]{:S(2)}) async-start(bf16[32,16,1152]{2,1,0:T(8,128)(2,1)} %get-tuple-element.24), calls=%async_computation | async-start | bytes 2359296 | tf_op jit(solution)/shard_map/all_to_all | solution.py:391
  53.6 0.6 divide_subtract_fusion.1
  54.2 0.6 divide_subtract_fusion
  54.9 0.0 copy-done.4
  54.9 0.6 subtract_convert_fusion.2
  55.5 0.0 copy-done.1
  55.6 7.9 %fusion.8 = (f32[1,512,1152]{2,1,0:T(8,128)}, bf16[1,512,1152]{2,1,0:T(8,128)(2,1)}, f32[1,512,1152]{2,1,0:T(8,128)}) fusion(f32[1,512,1152]{2,1,0:T(8,128)} %param.33, f32[1,512,1152]{2,1,0:T(8,128)} %param.32, bf16[1,512,1152]{2,1,0:T(8,128)(2,1)S(1)} %copy-done.1, bf16[512,512]{1,0:T(8,128)(2,1)} %get-tuple-element.30, ...), kind=kOutput, calls=%fused_computation.17 | convolution fusion | flops 612237312 | bytes 13500416 | tf_op jit(solution)/shard_map/dot_general | solution.py:405
  63.5 0.0 copy-done.15
  63.5 4.8 %fusion.9 = (f32[1,1152,512]{2,1,0:T(8,128)}, bf16[1,1152,512]{2,1,0:T(8,128)(2,1)}, f32[1,1152,512]{2,1,0:T(8,128)}) fusion(f32[1,1152,512]{2,1,0:T(8,128)S(1)} %copy-done.15, f32[1,1152,512]{2,1,0:T(8,128)S(1)} %copy-done.16, bf16[1,1152,512]{2,1,0:T(8,128)(2,1)S(1)} %copy-done.2, bf16[512,1152]{1,0:T(8,128)(2,1)S(1)} %copy-done.17, ...), kind=kOutput, calls=%fused_computation.18 | convolution fusion | flops 612237312 | bytes 13500416 | tf_op jit(solution)/shard_map/dot_general | solution.py:406
  68.2 15.6 %all-to-all-done = bf16[32,16,1152]{2,1,0:T(8,128)(2,1)S(1)} async-done(((bf16[32,16,1152]{2,1,0:T(8,128)(2,1)}), bf16[32,16,1152]{2,1,0:T(8,128)(2,1)S(1)}, u32[]{:S(2)}, u32[]{:S(2)}) %all-to-all-start) | async-done | bytes 1179680 | tf_op jit(solution)/shard_map/all_to_all | solution.py:391
  83.8 1.4 %convolution_convert_fusion = bf16[256,1152]{1,0:T(8,128)(2,1)} fusion(bf16[512,1152]{1,0:T(8,128)(2,1)S(1)} %bitcast.49, s32[256]{0:T(256)S(1)} %convert_add_fusion), kind=kOutput, calls=%fused_computation.4 | convolution fusion | flops 302415872 | bytes 1770496 | tf_op jit(solution)/shard_map/dot_general | solution.py:398
  (29 shorter events, 0.1 us)
Async XLA Ops:
  0.6 3.1 %copy-start = (bf16[256,1152]{1,0:T(8,128)(2,1)S(1)}, bf16[256,1152]{1,0:T(8,128)(2,1)}, u32[]{:S(2)}) copy-start(bf16[256,1152]{1,0:T(8,128)(2,1)} %param.17) | copy-start | bytes 1769476
  5.3 48.2 %copy-start.5 = (f32[1,512]{1,0:T(1,128)S(1)}, f32[1,512]{1,0:T(1,128)}, u32[]{:S(2)}) copy-start(f32[1,512]{1,0:T(1,128)} %bias_ref.1) | copy-start | bytes 6148
  5.3 48.2 %copy-start.12 = (f32[1,512]{1,0:T(1,128)S(1)}, f32[1,512]{1,0:T(1,128)}, u32[]{:S(2)}) copy-start(f32[1,512]{1,0:T(1,128)} %param.30) | copy-start | bytes 6148
  5.3 48.3 %copy-start.13 = (f32[1,512]{1,0:T(1,128)S(1)}, f32[1,512]{1,0:T(1,128)}, u32[]{:S(2)}) copy-start(f32[1,512]{1,0:T(1,128)} %param.31) | copy-start | bytes 6148
  5.3 48.9 %copy-start.3 = (f32[1152]{0:T(1024)S(1)}, f32[1152]{0:T(1024)}, u32[]{:S(2)}) copy-start(f32[1152]{0:T(1024)} %param.19) | copy-start | bytes 13828
  5.3 48.9 %copy-start.6 = (f32[1152]{0:T(1024)S(1)}, f32[1152]{0:T(1024)}, u32[]{:S(2)}) copy-start(f32[1152]{0:T(1024)} %param.20) | copy-start | bytes 13828
  5.3 48.9 %copy-start.7 = (f32[1152]{0:T(1024)S(1)}, f32[1152]{0:T(1024)}, u32[]{:S(2)}) copy-start(f32[1152]{0:T(1024)} %param.21) | copy-start | bytes 13828
  5.3 49.5 %copy-start.4 = (bf16[1,1152]{1,0:T(2,128)(2,1)S(1)}, bf16[1,1152]{1,0:T(2,128)(2,1)}, u32[]{:S(2)}) copy-start(bf16[1,1152]{1,0:T(2,128)(2,1)} %router_ref.1) | copy-start | bytes 6916
  5.4 49.5 %copy-start.9 = (f32[1,1152]{1,0:T(1,128)S(1)}, f32[1,1152]{1,0:T(1,128)}, u32[]{:S(2)}) copy-start(f32[1,1152]{1,0:T(1,128)} %param.23) | copy-start | bytes 13828
  5.4 49.5 %copy-start.10 = (f32[1,1152]{1,0:T(1,128)S(1)}, f32[1,1152]{1,0:T(1,128)}, u32[]{:S(2)}) copy-start(f32[1,1152]{1,0:T(1,128)} %param.24) | copy-start | bytes 13828
  5.4 50.1 %copy-start.1 = (bf16[1,512,1152]{2,1,0:T(8,128)(2,1)S(1)}, bf16[1,512,1152]{2,1,0:T(8,128)(2,1)}, u32[]{:S(2)}) copy-start(bf16[1,512,1152]{2,1,0:T(8,128)(2,1)} %param.27) | copy-start | bytes 3538948
  50.8 2.7 %copy-start.14 = (f32[1,512]{1,0:T(1,128)S(1)}, f32[1,512]{1,0:T(1,128)}, u32[]{:S(2)}) copy-start(f32[1,512]{1,0:T(1,128)} %get-tuple-element.29) | copy-start | bytes 6148
  50.8 3.3 %copy-start.8 = (f32[1,1152]{1,0:T(1,128)S(1)}, f32[1,1152]{1,0:T(1,128)}, u32[]{:S(2)}) copy-start(f32[1,1152]{1,0:T(1,128)} %get-tuple-element.25) | copy-start | bytes 13828
  50.9 4.0 %copy-start.11 = (f32[1,1152]{1,0:T(1,128)S(1)}, f32[1,1152]{1,0:T(1,128)}, u32[]{:S(2)}) copy-start(f32[1,1152]{1,0:T(1,128)} %get-tuple-element.26) | copy-start | bytes 13828
  50.9 33.0 %all-to-all-start = ((bf16[32,16,1152]{2,1,0:T(8,128)(2,1)}), bf16[32,16,1152]{2,1,0:T(8,128)(2,1)S(1)}, u32[]{:S(2)}, u32[]{:S(2)}) async-start(bf16[32,16,1152]{2,1,0:T(8,128)(2,1)} %get-tuple-element.24), calls=%async_computation | async-start | bytes 2359296 | tf_op jit(solution)/shard_map/all_to_all | solution.py:391
  55.5 7.9 %copy-start.2 = (bf16[1,1152,512]{2,1,0:T(8,128)(2,1)S(1)}, bf16[1,1152,512]{2,1,0:T(8,128)(2,1)}, u32[]{:S(2)}) copy-start(bf16[1,1152,512]{2,1,0:T(8,128)(2,1)} %param.25) | copy-start | bytes 3538948
  55.5 7.9 %copy-start.15 = (f32[1,1152,512]{2,1,0:T(8,128)S(1)}, f32[1,1152,512]{2,1,0:T(8,128)}, u32[]{:S(2)}) copy-start(f32[1,1152,512]{2,1,0:T(8,128)} %param.29) | copy-start | bytes 7077892
  55.5 7.9 %copy-start.16 = (f32[1,1152,512]{2,1,0:T(8,128)S(1)}, f32[1,1152,512]{2,1,0:T(8,128)}, u32[]{:S(2)}) copy-start(f32[1,1152,512]{2,1,0:T(8,128)} %param.28) | copy-start | bytes 7077892
  55.5 7.9 %copy-start.17 = (bf16[512,1152]{1,0:T(8,128)(2,1)S(1)}, bf16[512,1152]{1,0:T(8,128)(2,1)}, u32[]{:S(2)}) copy-start(bf16[512,1152]{1,0:T(8,128)(2,1)} %get-tuple-element.27) | copy-start | bytes 3538948
  55.5 7.9 %copy-start.18 = (bf16[512,512]{1,0:T(8,128)(2,1)S(1)}, bf16[512,512]{1,0:T(8,128)(2,1)}, u32[]{:S(2)}) copy-start(bf16[512,512]{1,0:T(8,128)(2,1)} %get-tuple-element.28) | copy-start | bytes 1572868
